TPU v7x, 128 devices: a whole 4x4x4 slice. The times are simulated.
128 devices in a mesh: seq: 32 (over z, y, core), dp: 4 (over x).
Axes of the slice: x: 4, y: 4, z: 4, core: 2. Of those that a mesh axis runs over, the one named last changes fastest.
Arguments:
- resid: bfloat16 [4, 16384, 2048], P('dp', 'seq'), may hold values from -6 to 6
- token_ids: int32 [4, 16384], P('dp', 'seq'), may hold values from 0 to 63999
- code_proj: float32 [6, 2048], replicated, may hold values from -2.5 to 2.5
- w_query: bfloat16 [2048, 1024], replicated, may hold values from -0.125 to 0.125
- w_key: bfloat16 [2048, 1024], replicated, may hold values from -0.125 to 0.125
- w_value: bfloat16 [2048, 1024], replicated, may hold values from -0.125 to 0.125
- gain: float32 [1024], replicated, may hold values from 0.1 to 1.9
- out_grad: bfloat16 [4, 16384, 1024], P('dp', 'seq'), may hold values from -6 to 6
Outputs:
- resid_grad: bfloat16 [4, 16384, 2048], P('dp', 'seq')
- weight_grads: float32 [2048, 3, 1024], P(('seq', 'dp'))
- gain_grad: float32 [1024], replicated
- code_grad: float32 [6, 2048], replicated
Inputs may be any that keep to these rules, and one draw needn't show every extreme that they name: `token_ids`: ids of the codebook of 64000 codes.
All inputs are finite; a program needn't handle non-finite values.
Results may differ from a plain program's by a relative error of at most 0.0084.
Values sent between devices are 32-bit elements; how exact they have to be, the bound alone decides.
A program may use at most 128 MiB of HBM per device.

v0:
```python
import functools
import math

import jax
import jax.numpy as jnp
from jax import lax
from jax.sharding import Mesh
from jax.sharding import PartitionSpec as P

HEADS = 8
DH = 128
SEQ = ("seq_0", "seq_1", "seq_2")
SEQ_DP = ("seq_0", "seq_1", "seq_2", "dp")


fsq_levels = (8, 8, 8, 5, 5, 5)
fsq_bases = (1, 8, 64, 512, 2560, 12800)


def neutral_like(shard, identity):
    return jnp.zeros_like(shard) + jnp.asarray(identity, shard.dtype)


def carried_in(shard, axes, combine, identity, reverse):
    before = start = neutral_like(shard, identity)
    running = shard
    for axis in reversed(axes):
        count, place = (lax.axis_size(axis), lax.axis_index(axis))
        pieces = lax.all_gather(running, axis)
        inside, running = (start, start)
        for k in reversed(range(count)) if reverse else range(count):
            passed = k > place if reverse else k < place
            running = combine(running, pieces[k])
            inside = jnp.where(passed, running, inside)
        before = combine(inside, before)
    return before


def one_axis_at_a_time(shard, axes):
    return functools.reduce(lax.psum, axes, shard)


def split_up(shard, dim, count):
    shape = shard.shape
    parts = shard.reshape(*shape[:dim], count, shape[dim] // count, *shape[dim + 1 :])
    return jnp.moveaxis(parts, dim, 0)


def sum_at_owner(shard, axis, dim):
    parts = split_up(shard, dim, lax.axis_size(axis))
    arrived = lax.all_to_all(parts, axis, split_axis=0, concat_axis=0, tiled=True)
    return arrived.sum(axis=0)


def code_rows(token_ids):
    code_list = []
    for fsq_level, fsq_base in zip(fsq_levels, fsq_bases):
        fsq_digit = token_ids // fsq_base % fsq_level
        code_list.append((2.0 * fsq_digit.astype(jnp.float32) - (fsq_level - 1)) / (fsq_level - 1))
    return jnp.stack(code_list)


def silu_slope(value):
    sigma = jax.nn.sigmoid(value)
    return sigma * (1.0 + value * (1.0 - sigma))


def add_states(earlier, later):
    return earlier + later


def body(resid, token_ids, code_proj, w_query, w_key, w_value, gain, out_grad):
    f32 = jnp.float32
    positions = resid.shape[1]
    code_values = code_rows(token_ids[0])
    summed = resid[0].astype(f32)
    for index in range(code_values.shape[0]):
        summed = summed + code_values[index][:, None] * code_proj[index]
    inputs = summed.astype(jnp.bfloat16)
    query_pre = jnp.dot(inputs, w_query, preferred_element_type=f32)
    key_pre = jnp.dot(inputs, w_key, preferred_element_type=f32)
    value_pre = jnp.dot(inputs, w_value, preferred_element_type=f32)

    def to_heads(array):
        return array.reshape(positions, HEADS, DH).transpose(1, 0, 2)

    def from_heads(array):
        return array.transpose(1, 0, 2).reshape(positions, HEADS * DH)

    queries = to_heads(jax.nn.silu(query_pre).astype(jnp.bfloat16))
    keys = to_heads(jax.nn.silu(key_pre).astype(jnp.bfloat16))
    values = to_heads(value_pre.astype(jnp.bfloat16))
    grads_out = to_heads(out_grad[0])
    block_kv = jnp.einsum("hte,htd->hed", keys, values, preferred_element_type=f32)
    empty_state = jnp.zeros_like(block_kv)
    prefix = carried_in(block_kv, SEQ, add_states, empty_state, False).astype(jnp.bfloat16)
    row_ids = lax.broadcasted_iota(jnp.int32, (positions, positions), 0)
    col_ids = lax.broadcasted_iota(jnp.int32, (positions, positions), 1)
    causal = col_ids <= row_ids
    scores = jnp.where(
        causal, jnp.einsum("hte,hse->hts", queries, keys, preferred_element_type=f32), 0.0
    ).astype(jnp.bfloat16)
    attended = jnp.einsum("hts,hsd->htd", scores, values, preferred_element_type=f32)
    attended = attended + jnp.einsum("hte,hed->htd", queries, prefix, preferred_element_type=f32)
    root = jnp.sqrt(jnp.mean(attended * attended, axis=-1, keepdims=True) + 1e-06)
    normed = attended / root
    d_normed = grads_out.astype(f32) * gain.reshape(HEADS, 1, DH)
    d_att = (
        (d_normed - normed * jnp.mean(d_normed * normed, axis=-1, keepdims=True)) / root
    ).astype(jnp.bfloat16)
    gain_term = jnp.sum(grads_out.astype(f32) * normed, axis=1).reshape(HEADS * DH)
    block_grad = jnp.einsum("hte,htd->hed", queries, d_att, preferred_element_type=f32)
    suffix = carried_in(block_grad, SEQ, add_states, empty_state, True).astype(jnp.bfloat16)
    back_scores = jnp.where(
        causal, jnp.einsum("htd,hsd->hts", d_att, values, preferred_element_type=f32), 0.0
    ).astype(jnp.bfloat16)
    d_query = jnp.einsum("hts,hse->hte", back_scores, keys, preferred_element_type=f32)
    d_query = d_query + jnp.einsum("htd,hed->hte", d_att, prefix, preferred_element_type=f32)
    d_key = jnp.einsum("hts,hte->hse", back_scores, queries, preferred_element_type=f32)
    d_key = d_key + jnp.einsum("hsd,hed->hse", values, suffix, preferred_element_type=f32)
    d_value = jnp.einsum("hts,htd->hsd", scores, d_att, preferred_element_type=f32)
    d_value = d_value + jnp.einsum("hse,hed->hsd", keys, suffix, preferred_element_type=f32)
    grad_q = (from_heads(d_query) * silu_slope(query_pre)).astype(jnp.bfloat16)
    grad_k = (from_heads(d_key) * silu_slope(key_pre)).astype(jnp.bfloat16)
    grad_v = from_heads(d_value).astype(jnp.bfloat16)
    transpose_dims = (((1,), (1,)), ((), ()))
    input_grad = lax.dot_general(grad_q, w_query, transpose_dims, preferred_element_type=f32)
    input_grad = input_grad + lax.dot_general(
        grad_k, w_key, transpose_dims, preferred_element_type=f32
    )
    input_grad = input_grad + lax.dot_general(
        grad_v, w_value, transpose_dims, preferred_element_type=f32
    )
    resid_grad = input_grad.astype(jnp.bfloat16)[None]
    all_tokens = positions * lax.axis_size(SEQ) * lax.axis_size("dp")
    grad_scale = 1.0 / math.sqrt(all_tokens)
    code_term = jnp.dot(code_values, input_grad, precision=lax.Precision.HIGHEST)
    gain_sum, code_sum = (
        one_axis_at_a_time(gain_term, SEQ_DP),
        one_axis_at_a_time(code_term, SEQ_DP),
    )
    row_dims = (((0,), (0,)), ((), ()))
    products = [
        lax.dot_general(inputs, grad_part, row_dims, preferred_element_type=f32)
        for grad_part in (grad_q, grad_k, grad_v)
    ]
    seq_summed = lax.psum_scatter(jnp.stack(products, axis=1), SEQ, scatter_dimension=0, tiled=True)
    weight_sum = sum_at_owner(seq_summed, "dp", 0)
    return (resid_grad, weight_sum * grad_scale, gain_sum * grad_scale, code_sum * grad_scale)


def solution(mesh):
    finer = Mesh(mesh.devices.reshape(4, 4, 2, mesh.shape["dp"]), ("seq_0", "seq_1", "seq_2", "dp"))
    return jax.shard_map(
        body,
        mesh=finer,
        in_specs=(P("dp", SEQ, None), P("dp", SEQ), P(), P(), P(), P(), P(), P("dp", SEQ, None)),
        out_specs=(P("dp", SEQ, None), P(SEQ_DP, None, None), P(), P()),
        check_vma=False,
    )
```

profile of v0, /device:TPU:0, one launch (start us, length us, event | category | flops | bytes accessed | tf_op | source)
XLA Modules:
  0.0 388.3 jit_solution(16337950225822163911)
XLA Ops:
  9.1 3.9 %fusion.6 = bf16[512,2048]{1,0:T(8,128)(2,1)S(1)} fusion(bf16[1,512,2048]{2,1,0:T(8,128)(2,1)} %param.8, f32[2048]{0:T(1024)S(1)} %bitcast.189, f32[512]{0:T(512)S(1)} %get-tuple-element.30, f32[2048]{0:T(1024)S(1)} %bitcast.191, f32[512]{0:T(512)S(1)} %get-tuple-element.28, f32[2048]{0:T(1024)S(1)} %bitcast.183, f32[512]{0:T(512)S(1)} %get-tuple-element.29, ...), kind=kLoop, calls=%fused_computation.14 | loop fusion | flops 14680064 | bytes 4255744 | tf_op jit(solution)/shard_map/convert_element_type | solution.py:79
  13.0 2.4 convolution_convert_fusion
  15.9 3.8 multiply_convert_fusion.2
  22.1 1.5 fusion.27
  23.7 14.3 %all-gather.15.cloned.1.call-done = f32[16,128,128]{2,1,0:T(8,128)} async-done(((f32[8,128,128]{2,1,0:T(8,128)}), f32[16,128,128]{2,1,0:T(8,128)}) %all-gather.15.cloned.1.call-update) | async-done | bytes 1048592 | tf_op jit(solution)/shard_map/all_gather | solution.py:29
  38.0 2.1 slice_add_fusion.13
  40.1 32.3 %all-gather.19.cloned.1.call-done = f32[32,128,128]{2,1,0:T(8,128)} async-done(((f32[8,128,128]{2,1,0:T(8,128)}), f32[32,128,128]{2,1,0:T(8,128)}) %all-gather.19.cloned.1.call-update) | async-done | bytes 2097168 | tf_op jit(solution)/shard_map/all_gather | solution.py:29
  72.4 2.4 fusion.45
  76.6 1.5 copy.28
  78.1 7.1 %multiply_convert_fusion.3 = (bf16[512,1024]{1,0:T(8,128)(2,1)}, f32[512,1024]{1,0:T(8,128)}) fusion(bf16[512,2048]{1,0:T(8,128)(2,1)} %copy-done.18, bf16[2048,1024]{1,0:T(8,128)(2,1)} %param.11), kind=kOutput, calls=%fused_computation.45 | convolution fusion | flops 2150105088 | bytes 9437184 | tf_op jit(solution)/shard_map/dot_general | solution.py:80
  85.2 1.5 copy.55
  86.9 2.7 select_convert_fusion.1
  89.6 1.9 copy-done
  91.6 2.8 fusion.28
  94.4 11.6 %all-gather.11.cloned.1.call-done = f32[4,8,128,128]{3,2,1,0:T(8,128)} async-done(((f32[1,8,128,128]{3,2,1,0:T(8,128)}), f32[4,8,128,128]{3,2,1,0:T(8,128)}) %all-gather.11.cloned.1.call-update) | async-done | bytes 2097168 | tf_op jit(solution)/shard_map/all_gather | solution.py:29
  105.9 3.2 fusion.44
  113.4 11.7 %all-gather.17.cloned.1.call-done = f32[16,128,128]{2,1,0:T(8,128)} async-done(((f32[8,128,128]{2,1,0:T(8,128)}), f32[16,128,128]{2,1,0:T(8,128)}) %all-gather.17.cloned.1.call-update) | async-done | bytes 1048592 | tf_op jit(solution)/shard_map/all_gather | solution.py:29
  125.1 2.1 slice_add_fusion.6
  127.3 32.3 %all-gather.21.cloned.1.call-done = f32[32,128,128]{2,1,0:T(8,128)} async-done(((f32[8,128,128]{2,1,0:T(8,128)}), f32[32,128,128]{2,1,0:T(8,128)}) %all-gather.21.cloned.1.call-update) | async-done | bytes 2097168 | tf_op jit(solution)/shard_map/all_gather | solution.py:29
  159.5 2.4 fusion.41
  162.2 2.4 select_convert_fusion
  164.7 1.5 fusion.32
  166.7 1.8 convolution_add_fusion
  168.5 2.9 copy.62
  171.4 4.6 %fusion.116 = f32[8,512,128]{1,2,0:T(8,128)} fusion(bf16[8,512,128]{1,2,0:T(8,128)(2,1)S(1)} %copy-done.5, bf16[8,512,512]{2,1,0:T(8,128)(2,1)} %copy-done), kind=kOutput, calls=%fused_computation.217 | convolution fusion | flops 536870912 | bytes 7340032 | tf_op jit(solution)/shard_map/hts,htd->hsd/dot_general | solution.py:121
  176.0 2.1 fusion.115
  180.8 5.7 %convolution_bitcast_fusion.2 = f32[2048,1,1024]{2,0,1:T(8,128)} fusion(bf16[512,2048]{1,0:T(8,128)(2,1)S(1)} %copy-done.19, bf16[512,1024]{1,0:T(8,128)(2,1)S(1)} %multiply_convert_fusion.1), kind=kOutput, calls=%fused_computation.7 | convolution fusion | flops 2147483648 | bytes 11534336 | tf_op jit(solution)/shard_map/dot_general | solution.py:144
  186.4 6.7 %all-gather.13.cloned.1.call-done = f32[4,8,128,128]{3,2,1,0:T(8,128)} async-done(((f32[1,8,128,128]{3,2,1,0:T(8,128)}), f32[4,8,128,128]{3,2,1,0:T(8,128)}) %all-gather.13.cloned.1.call-update) | async-done | bytes 2097168 | tf_op jit(solution)/shard_map/all_gather | solution.py:29
  193.1 3.0 fusion.40
  196.2 1.5 add_convert_fusion
  198.4 1.9 convolution_add_fusion.1
  200.2 2.2 copy.63
  202.5 5.7 %convolution_bitcast_fusion = f32[2048,1,1024]{2,0,1:T(8,128)S(1)} fusion(bf16[512,1024]{0,1:T(8,128)(2,1)S(1)} %bitcast.178, bf16[1,512,2048]{2,1,0:T(8,128)(2,1)} %param.8, f32[2048]{0:T(1024)S(1)} %bitcast.190, f32[512]{0:T(512)S(1)} %get-tuple-element.30, f32[2048]{0:T(1024)S(1)} %bitcast.192, f32[512]{0:T(512)S(1)} %get-tuple-element.28, ...), kind=kOutput, calls=%fused_computation.5 | convolution fusion | flops 2162163712 | bytes 11595776 | tf_op jit(solution)/shard_map/dot_general | solution.py:144
  210.0 2.4 convolution_bitcast_fusion.1
  212.4 8.9 %pad_maximum_fusion = f32[2048,3,1024]{2,0,1:T(8,128)} fusion(f32[2048,1,1024]{2,0,1:T(8,128)S(1)} %convolution_bitcast_fusion, f32[2048,1,1024]{2,0,1:T(8,128)S(1)} %convolution_bitcast_fusion.1, f32[2048,1,1024]{2,0,1:T(8,128)S(1)} %bitcast.172), kind=kLoop, calls=%fused_computation | loop fusion | flops 12582912 | bytes 50331648 | tf_op jit(solution)/shard_map/stack | solution.py:147
  222.6 4.7 %fusion.111 = f32[512,2048]{1,0:T(8,128)S(1)} fusion(bf16[512,1024]{1,0:T(8,128)(2,1)S(1)} %copy-done.24, bf16[2048,1024]{1,0:T(8,128)(2,1)} %param.11), kind=kOutput, calls=%fused_computation.212 | convolution fusion | flops 2147483648 | bytes 9437184 | tf_op jit(solution)/shard_map/dot_general | solution.py:127
  227.3 2.4 fusion.113
  229.7 2.6 add_add_fusion
  232.3 2.1 fusion.114
  234.4 16.0 %all-reduce.2 = (f32[1024]{0:T(1024)S(1)}, f32[6,2048]{1,0:T(8,128)S(1)}) all-reduce(f32[1024]{0:T(1024)S(1)} %bitcast.193, f32[6,2048]{1,0:T(8,128)S(1)} %fusion.114), channel_id=1, replica_groups=mesh['seq_0'=4,'seq_1'=4,'seq_2'=2,'dp'=4] {'seq_0'}, use_global_device_ids=true, to_apply=%region_5.6 | all-reduce | flops 13312 | bytes 106496 | tf_op jit(solution)/shard_map/psum | solution.py:40
  250.4 17.8 %all-reduce.1 = (f32[1024]{0:T(1024)S(1)}, f32[6,2048]{1,0:T(8,128)S(1)}) all-reduce(f32[1024]{0:T(1024)S(1)} %get-tuple-element.10, f32[6,2048]{1,0:T(8,128)S(1)} %get-tuple-element.11), channel_id=1, replica_groups=mesh['seq_0'=4,'seq_1'=4,'seq_2'=2,'dp'=4] {'seq_1'}, use_global_device_ids=true, to_apply=%region_6.7 | all-reduce | flops 13312 | bytes 106496 | tf_op jit(solution)/shard_map/psum | solution.py:40
  268.2 3.6 all-reduce.3
  271.7 17.7 %all-reduce = (f32[1024]{0:T(1024)S(1)}, f32[6,2048]{1,0:T(8,128)S(1)}) all-reduce(f32[1024]{0:T(1024)S(1)} %get-tuple-element.12, f32[6,2048]{1,0:T(8,128)S(1)} %get-tuple-element.13), channel_id=1, replica_groups=mesh['seq_0'=4,'seq_1'=4,'seq_2'=2,'dp'=4] {'dp'}, use_global_device_ids=true, to_apply=%region_8.9 | all-reduce | flops 13312 | bytes 106496 | tf_op jit(solution)/shard_map/psum | solution.py:40
  290.7 71.6 %reduce-scatter.2.cloned.1.call-done = f32[64,3,1024]{2,0,1:T(8,128)} async-done(((f32[2048,3,1024]{2,0,1:T(8,128)}), f32[64,3,1024]{2,0,1:T(8,128)}) %reduce-scatter.2.cloned.1.call-update) | async-done | bytes 786448 | tf_op jit(solution)/shard_map/reduce_scatter | solution.py:147
  362.4 2.1 copy.44
  364.5 4.2 %all-to-all-start = ((f32[4,16,3,1024]{3,1,2,0:T(8,128)}), f32[4,16,3,1024]{3,1,2,0:T(8,128)S(1)}, u32[]{:S(2)}, u32[]{:S(2)}) async-start(f32[4,16,3,1024]{3,1,2,0:T(8,128)} %copy.44), calls=%async_computation.1 | async-start | bytes 1572864 | tf_op jit(solution)/shard_map/all_to_all | solution.py:51
  368.7 3.8 convert_bitcast_fusion.1
  372.5 8.0 %all-to-all-done = f32[4,16,3,1024]{3,1,2,0:T(8,128)S(1)} async-done(((f32[4,16,3,1024]{3,1,2,0:T(8,128)}), f32[4,16,3,1024]{3,1,2,0:T(8,128)S(1)}, u32[]{:S(2)}, u32[]{:S(2)}) %all-to-all-start) | async-done | bytes 786464 | tf_op jit(solution)/shard_map/all_to_all | solution.py:51
  (107 shorter events, 20.3 us)
Async XLA Ops:
  7.2 30.8 %all-gather.15.cloned.1.call-start = ((), (), s32[]{:S(2)}) async-start(), calls=%async_computation.5 | async-start | bytes 1572864 | tf_op jit(solution)/shard_map/all_gather | solution.py:29
  9.1 3.9 %copy-start.33 = (bf16[2048,1024]{1,0:T(8,128)(2,1)S(1)}, bf16[2048,1024]{1,0:T(8,128)(2,1)}, u32[]{:S(2)}) copy-start(bf16[2048,1024]{1,0:T(8,128)(2,1)} %param.13) | copy-start | bytes 12582916
  13.0 2.4 copy-start.18
  13.0 2.9 copy-start.31
  15.9 59.5 %copy-start.15 = (bf16[512,1024]{1,0:T(8,128)(2,1)}, bf16[512,1024]{1,0:T(8,128)(2,1)S(1)}, u32[]{:S(2)}) copy-start(bf16[512,1024]{1,0:T(8,128)(2,1)S(1)} %convolution_convert_fusion) | copy-start | bytes 3145732
  19.8 1.0 copy-start.10
  21.1 1.0 copy-start.12
  23.6 48.7 %all-gather.19.cloned.1.call-start = ((), (), s32[]{:S(2)}) async-start(), calls=%async_computation.7 | async-start | bytes 2621440 | tf_op jit(solution)/shard_map/all_gather | solution.py:29
  40.1 65.9 %all-gather.11.cloned.1.call-start = ((), (), s32[]{:S(2)}) async-start(), calls=%async_computation.2 | async-start | bytes 2621440 | tf_op jit(solution)/shard_map/all_gather | solution.py:29
  74.8 50.3 %all-gather.17.cloned.1.call-start = ((), (), s32[]{:S(2)}) async-start(), calls=%async_computation.6 | async-start | bytes 1572864 | tf_op jit(solution)/shard_map/all_gather | solution.py:29
  86.8 2.8 copy-start.28
  86.9 4.7 %copy-start.14 = (bf16[64,8,8,128]{3,2,1,0:T(8,128)(2,1)S(1)}, bf16[64,8,8,128]{3,2,1,0:T(8,128)(2,1)}, u32[]{:S(2)}) copy-start(bf16[64,8,8,128]{3,2,1,0:T(8,128)(2,1)} %copy.66) | copy-start | bytes 3145732
  89.6 2.0 copy-start
  105.9 3.2 copy-start.8
  109.1 0.7 copy-start.29
  111.1 1.0 copy-start.4
  113.4 46.1 %all-gather.21.cloned.1.call-start = ((), (), s32[]{:S(2)}) async-start(), calls=%async_computation.8 | async-start | bytes 2621440 | tf_op jit(solution)/shard_map/all_gather | solution.py:29
  127.2 35.0 %copy-start.5 = (bf16[8,512,128]{1,2,0:T(8,128)(2,1)S(1)}, bf16[8,512,128]{1,2,0:T(8,128)(2,1)}, u32[]{:S(2)}) copy-start(bf16[8,512,128]{1,2,0:T(8,128)(2,1)} %copy-done.4) | copy-start | bytes 3145732
  127.2 35.0 %copy-start.16 = (bf16[512,1024]{1,0:T(8,128)(2,1)S(1)}, bf16[512,1024]{1,0:T(8,128)(2,1)}, u32[]{:S(2)}) copy-start(bf16[512,1024]{1,0:T(8,128)(2,1)} %copy-done.15) | copy-start | bytes 3145732
  127.2 65.9 %all-gather.13.cloned.1.call-start = ((), (), s32[]{:S(2)}) async-start(), calls=%async_computation.3 | async-start | bytes 2621440 | tf_op jit(solution)/shard_map/all_gather | solution.py:29
  162.0 200.4 %reduce-scatter.2.cloned.1.call-start = ((), (), s32[]{:S(2)}) async-start(), calls=%async_computation.4 | async-start | bytes 25952256 | tf_op jit(solution)/shard_map/reduce_scatter | solution.py:147
  162.2 2.5 copy-start.13
  164.7 2.0 copy-start.1
  171.4 4.6 %copy-start.2 = (bf16[8,512,512]{2,1,0:T(8,128)(2,1)S(1)}, bf16[8,512,512]{2,1,0:T(8,128)(2,1)}, u32[]{:S(2)}) copy-start(bf16[8,512,512]{2,1,0:T(8,128)(2,1)} %copy-done.1) | copy-start | bytes 12582916
  176.0 2.1 copy-start.9
  176.0 3.0 copy-start.22
  179.0 1.8 copy-start.19
  179.8 1.0 copy-start.23
  186.4 9.7 %copy-start.6 = (f32[8,512,128]{1,2,0:T(8,128)S(1)}, f32[8,512,128]{1,2,0:T(8,128)}, u32[]{:S(2)}) copy-start(f32[8,512,128]{1,2,0:T(8,128)} %fusion.116) | copy-start | bytes 6291460
  186.4 9.7 %copy-start.11 = (bf16[512,1024]{1,0:T(8,128)(2,1)S(1)}, bf16[512,1024]{1,0:T(8,128)(2,1)}, u32[]{:S(2)}) copy-start(bf16[512,1024]{1,0:T(8,128)(2,1)} %copy-done.10) | copy-start | bytes 3145732
  196.1 1.8 copy-start.7
  196.1 2.2 copy-start.17
  200.2 2.2 copy-start.25
  202.5 5.7 %copy-start.21 = (f32[512,1024]{1,0:T(8,128)S(1)}, f32[512,1024]{1,0:T(8,128)}, u32[]{:S(2)}) copy-start(f32[512,1024]{1,0:T(8,128)} %get-tuple-element.35) | copy-start | bytes 6291460
  202.5 7.5 %copy-start.20 = (bf16[512,2048]{1,0:T(8,128)(2,1)S(1)}, bf16[512,2048]{1,0:T(8,128)(2,1)}, u32[]{:S(2)}) copy-start(bf16[512,2048]{1,0:T(8,128)(2,1)} %copy-done.18) | copy-start | bytes 6291460
  208.2 4.2 %slice-start = ((s8[8388608]{0:T(1024)(128)(4,1)}), s8[4194304]{0:T(1024)(128)(4,1)S(1)}, s32[]{:S(2)}) async-start(s8[8388608]{0:T(1024)(128)(4,1)} %bitcast.171), calls=%async_computation.9 | async-start | bytes 8388608
  209.0 1.0 copy-start.26
  210.0 2.4 slice-start.1
  221.3 0.7 copy-start.30
  221.3 1.2 copy-start.24
  222.6 4.7 %copy-start.27 = (bf16[512,1024]{1,0:T(8,128)(2,1)S(1)}, bf16[512,1024]{1,0:T(8,128)(2,1)}, u32[]{:S(2)}) copy-start(bf16[512,1024]{1,0:T(8,128)(2,1)} %copy-done.26) | copy-start | bytes 3145732
  222.6 4.7 %copy-start.32 = (bf16[2048,1024]{1,0:T(8,128)(2,1)S(1)}, bf16[2048,1024]{1,0:T(8,128)(2,1)}, u32[]{:S(2)}) copy-start(bf16[2048,1024]{1,0:T(8,128)(2,1)} %param.12) | copy-start | bytes 12582916
  227.3 2.4 copy-start.34
  232.3 2.1 copy-start.3
  364.5 16.0 %all-to-all-start = ((f32[4,16,3,1024]{3,1,2,0:T(8,128)}), f32[4,16,3,1024]{3,1,2,0:T(8,128)S(1)}, u32[]{:S(2)}, u32[]{:S(2)}) async-start(f32[4,16,3,1024]{3,1,2,0:T(8,128)} %copy.44), calls=%async_computation.1 | async-start | bytes 1572864 | tf_op jit(solution)/shard_map/all_to_all | solution.py:51
Sparse Core Ops, SparseCore 0:
  23.7 14.1 all-gather.14
  40.2 32.1 all-gather.18
  74.9 30.9 all-gather.10
  113.5 11.5 all-gather.16
  127.3 32.1 all-gather.20
  162.1 30.9 all-gather.12
  221.5 140.8 reduce-scatter.1
where the time goes:
time: 394 us; the launch traced here: 388 us
  waiting for transfers between devices  188 us (48%)
  matrix products  63.3 us (16%)
  blocking collectives  55 us (14%)
  other arithmetic  37.5 us (10%)
  local copies, waits for them, and re-layouts  23.9 us (6%)
  between operations  15 us (4%)
  starting transfers between devices  5.23 us (1%)
    all_gather x6, waiting for transfers between devices, carried_in(): pieces = lax.all_gather(running, axis)  109 us
    reduce_scatter x1, waiting for transfers between devices, body(): lax.psum_scatter(jnp.stack(products, axis=1), SEQ, scatter_dimension=0, t...  71.6 us
    psum x4, blocking collectives, one_axis_at_a_time(): return functools.reduce(lax.psum, axes, shard)  55 us
    dot_general x3, matrix products, body(): lax.dot_general(inputs, grad_part, row_dims, preferred_element_type=f32)  13.8 us
    unnamed x76, local copies, waits for them, and re-layouts  12.4 us
    add x4, other arithmetic, add_states(): return earlier + later  8.94 us
    another operation x1, other arithmetic, body(): jnp.stack(products, axis=1)  8.93 us
    all_to_all x1, waiting for transfers between devices, sum_at_owner(): lax.all_to_all(parts, axis, split_axis=0, concat_axis=0, tiled=True)  7.96 us
  transfers between devices with their start and end apart: 8, of which 8 were waited for; matrix products, arithmetic and copies ran while one was open for 14% of the time, Pallas kernels for 0%

commit v1 on v0

v1 whole, which is shorter than its diff:
```python
import functools
import math

import jax
import jax.numpy as jnp
from jax import lax
from jax.experimental import pallas as pl
from jax.experimental.pallas import tpu as pltpu
from jax.sharding import Mesh
from jax.sharding import PartitionSpec as P

HEADS = 8
DH = 128
T = 512
D = 2048
HALF = 512
ALL = ("z", "y", "c", "x")
MESH = pl.DeviceIdType.MESH
F32 = jnp.float32
BF16 = jnp.bfloat16

fsq_levels = (8, 8, 8, 5, 5, 5)
fsq_bases = (1, 8, 64, 512, 2560, 12800)

NT = (((1,), (1,)), ((), ()))
TN = (((0,), (0,)), ((), ()))


def dot(a, b, dims=None):
    if dims is None:
        return jnp.dot(a, b, preferred_element_type=F32)
    return lax.dot_general(a, b, dims, preferred_element_type=F32)


def entry_barrier(devices):
    barrier = pltpu.get_barrier_semaphore()
    for device in devices:
        pl.semaphore_signal(barrier, inc=1, device_id=device, device_id_type=MESH)
    pl.semaphore_wait(barrier, len(devices))


def send(src, dst, ssem, rsem, device):
    copy = pltpu.make_async_remote_copy(
        src_ref=src, dst_ref=dst, send_sem=ssem, recv_sem=rsem, device_id=device, device_id_type=MESH
    )
    copy.start()
    return copy


def ring(axis, step):
    return lax.rem(lax.axis_index(axis) + step, 4)


def m1_kernel(
    numt_ref, proj_ref, resid_ref, og_ref, gain_ref, wq_hbm, wk_hbm, wv_hbm,
    xt_ref, g_ref, numt_all, gain_out,
    wbuf, wsem, xs, xr, xssem, xrsem, gs, gr, gssem, grsem, ns, nr, nssem, nrsem,
    xb, q, k, v, sq, sk, og, sc, att, datt, dk, dv,
    blk, pre, ssend, srecv, s2send, s2recv, sssem, srsem,
):
    c = lax.axis_index("c")
    peer = {"c": 1 - c}
    y = lax.axis_index("y")
    z = lax.axis_index("z")
    own_col = pl.multiple_of(c * HALF, HALF)
    peer_col = pl.multiple_of((1 - c) * HALF, HALF)

    loads = []
    for n, w in enumerate((wk_hbm, wv_hbm, wq_hbm)):
        cp = pltpu.make_async_copy(w.at[:, pl.ds(own_col, HALF)], wbuf.at[n], wsem.at[n])
        cp.start()
        loads.append(cp)
    entry_barrier([peer] + [{"y": ring("y", s)} for s in (1, 2, 3)] + [{"z": ring("z", s)} for s in (1, 2, 3)])

    copies = []
    for r in range(2):
        rows = pl.ds(r * 256, 256)
        add = dot(numt_ref[:, rows], proj_ref[...], TN)
        x = (resid_ref[rows, :].astype(F32) + add).astype(BF16)
        xb[0, rows, :] = x
        xs[rows, :] = x.astype(F32)
        copies.append(send(xs.at[rows], xr.at[rows], xssem.at[r], xrsem.at[r], peer))
    gs[...] = og_ref[:, pl.ds(peer_col, HALF)].astype(F32)
    copies.append(send(gs, gr, gssem, grsem, peer))
    ns[...] = numt_ref[0:16, :].astype(F32)
    copies.append(send(ns, nr, nssem, nrsem, peer))

    def project(slot, n, base):
        for half in range(2):
            p = dot(xb[slot], wbuf[n, :, half * 256 : half * 256 + 256])
            for hh in range(2):
                a = p[:, hh * DH : hh * DH + DH]
                at = base + half * 2 + hh
                if n == 1:
                    v[at] = a.astype(BF16)
                else:
                    s = 1.0 / (1.0 + jnp.exp(-a))
                    slope = s * (1.0 + a * (1.0 - s))
                    if n == 0:
                        k[at] = (a * s).astype(BF16)
                        sk[at] = slope
                    else:
                        q[at] = (a * s).astype(BF16)
                        sq[at] = slope

    mine = c * 4
    other = (1 - c) * 4
    for n in range(3):
        loads[n].wait()
        project(0, n, mine)
    for h in range(4):
        og[mine + h] = og_ref[:, pl.ds(pl.multiple_of(c * HALF + h * DH, DH), DH)]
    for r in range(2):
        copies[r].wait()
        xb[1, pl.ds(r * 256, 256), :] = xr[pl.ds(r * 256, 256), :].astype(BF16)
    project(1, 0, other)
    project(1, 1, other)

    def scan_start(s):
        ssend[s, 0] = blk[s, 0, 0:2] + blk[s, 1, 0:2]
        ssend[s, 1] = blk[s, 0, 2:4] + blk[s, 1, 2:4]
        out = []
        for half, axis in ((0, "y"), (1, "z")):
            for d in (1, 2, 3):
                out.append(send(ssend.at[s, half], srecv.at[s, half, d - 1], sssem.at[s, 0, half, d - 1],
                                srsem.at[s, 0, half, d - 1], {axis: ring(axis, d)}))
        return out

    def before(place, d, s):
        return (d <= place) if s == 0 else (d > place)

    def scan_middle(s, sent):
        for cp in sent:
            cp.wait()
        total = ssend[s, 0]
        inside = jnp.zeros_like(total)
        for d in (1, 2, 3):
            piece = srecv[s, 0, d - 1]
            total = total + piece
            inside = inside + jnp.where(before(y, d, s), piece, 0.0)
        s2send[s, 0] = total
        pre[s, 0:2] = inside
        passed = jnp.zeros_like(total)
        for d in (1, 2, 3):
            passed = passed + jnp.where(before(z, d, s), srecv[s, 1, d - 1], 0.0)
        s2send[s, 1] = passed
        s2send[s, 2] = passed + ssend[s, 1]
        pre[s, 2:4] = passed
        out = []
        for d in (1, 2, 3):
            out.append(send(s2send.at[s, 0], s2recv.at[s, 0, d - 1], sssem.at[s, 1, 0, d - 1],
                            srsem.at[s, 1, 0, d - 1], {"z": ring("z", d)}))
            wraps = (y + d) // 4
            pick = 2 - wraps if s == 0 else 1 + wraps
            out.append(send(s2send.at[s, pick], s2recv.at[s, 1, d - 1], sssem.at[s, 1, 1, d - 1],
                            srsem.at[s, 1, 1, d - 1], {"y": ring("y", d)}))
        return out

    def scan_end(s, sent):
        for cp in sent:
            cp.wait()
        first = pre[s, 0:2]
        second = pre[s, 2:4]
        for d in (1, 2, 3):
            first = first + jnp.where(before(z, d, s), s2recv[s, 0, d - 1], 0.0)
            second = second + s2recv[s, 1, d - 1]
        pre[s, 0:2] = first
        pre[s, 2:4] = second

    def state(s, b, h):
        base = pre[s, h]
        if s == 0:
            return (base + jnp.where(b == 1, blk[0, 0, h], 0.0)).astype(BF16)
        return (base + jnp.where(b == 0, blk[1, 1, h], 0.0)).astype(BF16)

    def kv_step(n, _):
        blk[0, n // 4, lax.rem(n, 4)] = dot(k[n], v[n], TN)
        return 0

    lax.fori_loop(0, 8, kv_step, 0)
    sent = scan_start(0)
    project(1, 2, other)
    copies[2].wait()
    for h in range(4):
        og[other + h] = gr[:, h * DH : h * DH + DH].astype(BF16)
    copies[3].wait()
    numt_all[c] = numt_ref[0:16, :]
    numt_all[1 - c] = nr[...].astype(BF16)
    sent = scan_middle(0, sent)

    row_ids = lax.broadcasted_iota(jnp.int32, (T, T), 0)
    col_ids = lax.broadcasted_iota(jnp.int32, (T, T), 1)

    def score_step(n, _):
        s = jnp.where(col_ids <= row_ids, dot(q[n], k[n], NT), 0.0).astype(BF16)
        sc[n] = s
        att[n] = dot(s, v[n])
        return 0

    lax.fori_loop(0, 8, score_step, 0)
    scan_end(0, sent)

    def forward_step(n, _):
        b = n // 4
        h = lax.rem(n, 4)
        a = att[n] + dot(q[n], state(0, b, h))
        root = jnp.sqrt(jnp.mean(a * a, axis=-1, keepdims=True) + 1e-06)
        inv = 1.0 / root
        normed = a * inv
        g = og[n].astype(F32)
        dn = g * gain_ref[h]
        da = ((dn - normed * jnp.mean(dn * normed, axis=-1, keepdims=True)) * inv).astype(BF16)
        datt[n] = da
        att[n, 0:1, :] = jnp.sum(g * normed, axis=0, keepdims=True)
        blk[1, b, h] = dot(q[n], da, TN)
        return 0

    lax.fori_loop(0, 8, forward_step, 0)
    sent = scan_start(1)
    for h in range(4):
        gain_out[:, h * DH : h * DH + DH] = att[h, 0:1, :] + att[4 + h, 0:1, :]

    def put(kind, n, value):
        b = n // 4
        h = lax.rem(n, 4)
        g_ref[kind * 2 + h // 2, pl.ds(pl.multiple_of(b * T, T), T),
              pl.ds(pl.multiple_of(lax.rem(h, 2) * DH, DH), DH)] = value.astype(BF16)

    def back_step(n, _):
        b = n // 4
        h = lax.rem(n, 4)
        da = datt[n]
        bs = jnp.where(col_ids <= row_ids, dot(da, v[n], NT), 0.0).astype(BF16)
        dq = dot(bs, k[n]) + dot(da, state(0, b, h), NT)
        put(0, n, dq * sq[n])
        dk[n] = dot(bs, q[n], TN)
        dv[n] = dot(sc[n], da, TN)
        return 0

    lax.fori_loop(0, 4, back_step, 0)
    sent = scan_middle(1, sent)
    lax.fori_loop(4, 8, back_step, 0)

    def turn_step(n, _):
        cols = pl.ds(pl.multiple_of(n * 128, 128), 128)
        for slot in range(2):
            place = c if slot == 0 else 1 - c
            t = xb[slot, :, cols].T
            xt_ref[n // 4, lax.rem(n, 4), :, :, :, pl.ds(pl.multiple_of(place * T, T), T)] = t.reshape(2, 4, 16, T)
        return 0

    lax.fori_loop(0, 16, turn_step, 0)
    scan_end(1, sent)

    def last_step(n, _):
        st = state(1, n // 4, lax.rem(n, 4))
        put(1, n, (dk[n] + dot(v[n], st, NT)) * sk[n])
        put(2, n, dv[n] + dot(k[n], st))
        return 0

    lax.fori_loop(0, 8, last_step, 0)


PLAN = (("x", 1), ("x", -1), ("y", 1), ("z", 1), ("y", -1), ("z", -1))
ORDER = {"x": ("x", "z", "y"), "y": ("y", "x", "z"), "z": ("z", "y", "x")}
DIMS = {"x": (4, 4, 2), "y": (4, 2, 4), "z": (4, 2, 4)}
DIMS2 = {"x": (4, 2), "y": (4, 2), "z": (2, 4)}


def m2_kernel(
    scale, xt_ref, g_ref, numt_ref, gain_ref, lev_ref, wq_hbm, wk_hbm, wv_hbm,
    wout, rg_out, gain_out, code_out, *scr,
):
    wbuf, wsem, igs, igr, igo, igsem, ar, arr, arsem, fs, fr, fsem, ps, pr, psem, sems = scr[:16]
    tx, t2 = scr[16:22], scr[22:28]
    recv = [[scr[28 + 18 * phase + 6 * m : 34 + 18 * phase + 6 * m] for m in range(3)] for phase in range(3)]
    c = lax.axis_index("c")
    peer = {"c": 1 - c}
    own_col = pl.multiple_of(c * HALF, HALF)
    peer_col = pl.multiple_of((1 - c) * HALF, HALF)
    loads = []
    for n, w in enumerate((wq_hbm, wk_hbm, wv_hbm)):
        cp = pltpu.make_async_copy(w.at[:, pl.ds(own_col, HALF)], wbuf.at[n], wsem.at[n])
        cp.start()
        loads.append(cp)
    entry_barrier([peer] + [{a: ring(a, s)} for a in ("x", "y", "z") for s in (1, 3)])

    def lhs(axis, i):
        if axis == "x":
            rows = xt_ref[:, :, :, i]
        elif axis == "y":
            rows = xt_ref[:, i]
        else:
            rows = xt_ref[i]
        return rows.reshape(512, 1024)

    def product(hp, i):
        axis = PLAN[hp][0]
        return dot(lhs(axis, i), g_ref[hp]).reshape(*DIMS[axis], 16, 256)

    sends = {}

    def go(hp, phase, m, src, dirn):
        axis = ORDER[PLAN[hp][0]][phase]
        sends[hp, phase, m] = send(src, recv[phase][m][hp], sems.at[0, hp, phase, m], sems.at[1, hp, phase, m],
                                   {axis: ring(axis, 1 if dirn == 1 else 3)})

    order = (2, 3, 0, 4, 5, 1)
    for hp in order:
        axis, d = PLAN[hp]
        tx[hp][0] = product(hp, ring(axis, 2))
        go(hp, 0, 0, tx[hp].at[0], d)
    for hp in order:
        axis, d = PLAN[hp]
        tx[hp][1] = product(hp, ring(axis, 3 if d == 1 else 1))
        go(hp, 0, 1, tx[hp].at[1], -d)
    for cp in loads:
        cp.wait()

    def ig_step(n, target, base):
        rows = pl.ds(pl.multiple_of(base + n * 128, 128), 128)
        total = None
        for t in range(3):
            left = jnp.concatenate([g_ref[2 * t, rows, :], g_ref[2 * t + 1, rows, :]], axis=1)
            part = dot(left, wbuf[t], NT)
            total = part if total is None else total + part
        target[pl.ds(pl.multiple_of(n * 128, 128), 128), :] = total
        return 0

    for hp in order:
        axis, d = PLAN[hp]
        mid = product(hp, ring(axis, 1 if d == 1 else 3))
        sends[hp, 0, 0].wait_recv()
        recv[0][0][hp][...] = recv[0][0][hp][...] + mid
        go(hp, 0, 2, recv[0][0][hp], d)
    for hp in range(6):
        s = dot(numt_ref[0], g_ref[hp, 0:T, :]) + dot(numt_ref[1], g_ref[hp, T : 2 * T, :])
        ar[0, hp] = s[0:8]
    for hp in range(2):
        ar[0, hp, 6:7, :] = gain_ref[:, hp * 256 : hp * 256 + 256]
    steps = [(a, m) for a in ("x", "y", "z") for m in (0, 1)]

    def small(n):
        axis, m = steps[n]
        i = lax.axis_index(axis)
        partner = 3 - i if m else i + 1 - 2 * lax.rem(i, 2)
        return send(ar.at[n], arr.at[n], arsem.at[0, n], arsem.at[1, n], {axis: partner})

    small_copy = small(0)
    lax.fori_loop(0, 4, lambda n, _: ig_step(n, igs, (1 - c) * T), 0)
    ig_copy = send(igs, igr, igsem.at[0], igsem.at[1], peer)
    for hp in order:
        tx[hp][2] = product(hp, ring(PLAN[hp][0], 0))

    def small_next(n, cp):
        cp.wait()
        ar[n + 1] = ar[n] + arr[n]
        return small(n + 1) if n + 1 < 6 else None

    small_copy = small_next(0, small_copy)
    lax.fori_loop(0, 4, lambda n, _: ig_step(n, igo, c * T), 0)
    small_copy = small_next(1, small_copy)
    ig_copy.wait()
    rg_out[...] = (igo[...] + igr[...]).astype(BF16)
    for n in range(2, 6):
        small_copy = small_next(n, small_copy)

    code = jnp.zeros((8, D), F32)
    for hp in range(6):
        s = ar[6, hp]
        if hp < 2:
            ps[:, D + hp * 256 : D + hp * 256 + 256] = s
        s = s * lev_ref[...]
        for _ in range(3):
            part = s.astype(BF16)
            s = s - part.astype(F32)
            code = code + dot(part, wbuf[hp // 2, :, (hp % 2) * 256 : (hp % 2) * 256 + 256], NT)
    ps[:, 0:D] = code
    p_copy = send(ps, pr, psem.at[0], psem.at[1], peer)

    def piece(hp, phase, i):
        axis = PLAN[hp][0]
        if phase == 1:
            return tx[hp].at[2, :, :, i] if axis == "y" else tx[hp].at[2, i]
        return t2[hp].at[:, i] if axis == "z" else t2[hp].at[i]

    for phase in (1, 2):
        for hp in order:
            axis, d = ORDER[PLAN[hp][0]][phase], PLAN[hp][1]
            sends[hp, phase - 1, 1].wait_recv()
            sends[hp, phase - 1, 2].wait_recv()
            arrived = recv[phase - 1][1][hp][...] + recv[phase - 1][2][hp][...]
            if phase == 1:
                tx[hp][2] = tx[hp][2] + arrived
            else:
                t2[hp][...] = piece(hp, 1, ring(ORDER[PLAN[hp][0]][1], 0))[...] + arrived
            go(hp, phase, 0, piece(hp, phase, ring(axis, 2)), d)
            go(hp, phase, 1, piece(hp, phase, ring(axis, 3 if d == 1 else 1)), -d)
        for hp in order:
            axis, d = ORDER[PLAN[hp][0]][phase], PLAN[hp][1]
            sends[hp, phase, 0].wait_recv()
            relay = recv[phase][0][hp]
            relay[...] = relay[...] + piece(hp, phase, ring(axis, 1 if d == 1 else 3))[...]
            go(hp, phase, 2, relay, d)

    for hp in range(6):
        sends[hp, 2, 1].wait_recv()
        sends[hp, 2, 2].wait_recv()
        last = ORDER[PLAN[hp][0]][2]
        fs[:, :, hp * 256 : hp * 256 + 256] = (
            piece(hp, 2, ring(last, 0))[...] + recv[2][1][hp][...] + recv[2][2][hp][...]
        ) * scale
    f_copy = send(fs.at[1 - c], fr, fsem.at[0], fsem.at[1], peer)
    for t in range(3):
        wout[t, :, pl.ds(own_col, HALF)] = fs[c, :, t * HALF : t * HALF + HALF]
    p_copy.wait()
    code_out[...] = (ps[:, 0:D] + pr[:, 0:D]) * scale
    gain_out[:, pl.ds(own_col, HALF)] = ps[:, D:] * scale
    gain_out[:, pl.ds(peer_col, HALF)] = pr[:, D:] * scale
    f_copy.wait()
    for t in range(3):
        wout[t, :, pl.ds(peer_col, HALF)] = fr[:, t * HALF : t * HALF + HALF]
    for cp in sends.values():
        cp.wait_send()


def vmem(*shape, dtype=F32):
    return pltpu.VMEM(shape, dtype)


def body(resid, token_ids, code_proj, w_query, w_key, w_value, gain, out_grad):
    dma = pltpu.SemaphoreType.DMA
    levels = jnp.array(fsq_levels, jnp.int32)[:, None]
    bases = jnp.array(fsq_bases, jnp.int32)[:, None]
    nums = (2 * (token_ids // bases % levels) - (levels - 1)).astype(BF16)
    nums = jnp.pad(nums, ((0, 10), (0, 0)))
    inv = 1.0 / (jnp.array(fsq_levels, F32) - 1.0)[:, None]
    rest = code_proj * inv
    terms = []
    for _ in range(3):
        term = lax.reduce_precision(rest, 8, 7)
        terms.append(jnp.pad(term.astype(BF16), ((0, 10), (0, 0))))
        rest = rest - term
    proj3 = jnp.concatenate(terms, axis=0)
    numt = jnp.concatenate([nums, nums, nums], axis=0)
    c = lax.axis_index("c")
    gain_heads = lax.dynamic_slice(gain, (c * HALF,), (HALF,)).reshape(4, 1, DH)
    any_spec = pl.BlockSpec(memory_space=pl.ANY)
    vm = pl.BlockSpec(memory_space=pltpu.VMEM)
    sds = jax.ShapeDtypeStruct
    xt, g, numt_all, gain_row = pl.pallas_call(
        m1_kernel,
        name="m1",
        out_shape=(sds((4, 4, 2, 4, 16, 2 * T), BF16), sds((6, 2 * T, 256), BF16), sds((2, 16, T), BF16), sds((1, HALF), F32)),
        in_specs=[vm] * 5 + [any_spec] * 3,
        out_specs=(vm,) * 4,
        scratch_shapes=[
            vmem(3, D, HALF, dtype=BF16), dma((3,)),
            vmem(T, D), vmem(T, D), dma((2,)), dma((2,)),
            vmem(T, HALF), vmem(T, HALF), dma, dma,
            vmem(16, T), vmem(16, T), dma, dma,
            vmem(2, T, D, dtype=BF16),
            vmem(8, T, DH, dtype=BF16), vmem(8, T, DH, dtype=BF16), vmem(8, T, DH, dtype=BF16),
            vmem(8, T, DH), vmem(8, T, DH), vmem(8, T, DH, dtype=BF16), vmem(8, T, T, dtype=BF16),
            vmem(8, T, DH), vmem(8, T, DH, dtype=BF16), vmem(8, T, DH), vmem(8, T, DH),
            vmem(2, 2, 4, DH, DH), vmem(2, 4, DH, DH),
            vmem(2, 2, 2, DH, DH), vmem(2, 2, 3, 2, DH, DH), vmem(2, 3, 2, DH, DH), vmem(2, 2, 3, 2, DH, DH),
            dma((2, 2, 2, 3)), dma((2, 2, 2, 3)),
        ],
        compiler_params=pltpu.CompilerParams(collective_id=0, has_side_effects=True, vmem_limit_bytes=VMEM_LIMIT),
    )(numt, proj3, resid[0], out_grad[0], gain_heads, w_query, w_key, w_value)

    scale = 1.0 / math.sqrt(T * lax.axis_size(ALL))
    lev = jnp.pad(inv, ((0, 2), (0, 0)))
    lev = jnp.broadcast_to(lev, (8, 256))
    w_out, resid_grad, gain_out, code_out = pl.pallas_call(
        functools.partial(m2_kernel, scale),
        name="m2",
        out_shape=(sds((3, 16, 2 * HALF), F32), sds((T, D), BF16), sds((8, 2 * HALF), F32), sds((8, D), F32)),
        in_specs=[vm] * 5 + [any_spec] * 3,
        out_specs=(vm,) * 4,
        scratch_shapes=[
            vmem(3, D, HALF, dtype=BF16), dma((3,)),
            vmem(T, D), vmem(T, D), vmem(T, D), dma((2,)),
            vmem(7, 6, 8, 256), vmem(6, 6, 8, 256), dma((2, 6)),
            vmem(2, 16, 3 * HALF), vmem(16, 3 * HALF), dma((2,)),
            vmem(8, D + HALF), vmem(8, D + HALF), dma((2,)),
            dma((2, 6, 3, 3)),
            *[vmem(3, *DIMS[a], 16, 256) for a, _ in PLAN],
            *[vmem(*DIMS2[a], 16, 256) for a, _ in PLAN],
            *[vmem(*DIMS[a], 16, 256) for _ in range(3) for a, _ in PLAN],
            *[vmem(*DIMS2[a], 16, 256) for _ in range(3) for a, _ in PLAN],
            *[vmem(2, 16, 256) for _ in range(3) for a, _ in PLAN],
        ],
        compiler_params=pltpu.CompilerParams(collective_id=1, has_side_effects=True, vmem_limit_bytes=VMEM_LIMIT),
    )(xt, g, numt_all, gain_row, lev, w_query, w_key, w_value)
    return resid_grad[None], w_out.transpose(1, 0, 2), gain_out[6], code_out[0:6]


VMEM_LIMIT = 66_000_000


def solution(mesh):
    finer = Mesh(mesh.devices.reshape(4, 4, 2, 4), ALL)
    seq = ("z", "y", "c")
    return jax.shard_map(
        body,
        mesh=finer,
        in_specs=(P("x", seq, None), P("x", seq), P(), P(), P(), P(), P(), P("x", seq, None)),
        out_specs=(P("x", seq, None), P(ALL, None, None), P(), P()),
        check_vma=False,
    )
```

time: 394 us -> 168 us (0.43); the launches traced: 388 us -> 167 us
  waiting for transfers between devices: 188 us -> 0 us
  Pallas kernels: 0 us -> 154 us
  matrix products: 63.3 us -> 0 us
  blocking collectives: 55 us -> 0 us
  other arithmetic: 37.5 us -> 4.17 us
  local copies, waits for them, and re-layouts: 23.9 us -> 7.89 us
  between operations: 15 us -> 0.69 us
  starting transfers between devices: 5.23 us -> 0 us
    pallas_call x0 -> x2, Pallas kernels: none -> 154 us  [the longest x1 92.3 us: body(): pl.pallas_call(functools.partial(m2_kernel, scale), name='m2', out_shape=...]
    all_gather x6 -> x0, waiting for transfers between devices: 109 us -> none  [carried_in(): pieces = lax.all_gather(running, axis)]
    reduce_scatter x1 -> x0, waiting for transfers between devices: 71.6 us -> none  [body(): lax.psum_scatter(jnp.stack(products, axis=1), SEQ, scatter_dimension=0, t...]
    dot_general x22 -> x0, matrix products: 63.3 us -> none  [the longest x3 13.8 us: body(): lax.dot_general(inputs, grad_part, row_dims, preferred_element_type=f32)]
    psum x4 -> x0, blocking collectives: 55 us -> none  [one_axis_at_a_time(): return functools.reduce(lax.psum, axes, shard)]
    convert_element_type x6 -> x2, other arithmetic: 12.2 us -> 2.14 us  [the longest x1 1.22 us: body(): nums = (2 * (token_ids // bases % levels) - (levels - 1)).astype(BF16)]
    add x4 -> x0, other arithmetic: 8.94 us -> none  [add_states(): return earlier + later]
    another operation x1 -> x0, other arithmetic: 8.93 us -> none  [body(): jnp.stack(products, axis=1)]
  transfers between devices with their start and end apart: 8 -> 0, of which waited for: 8 -> 0; matrix products, arithmetic and copies ran while one was open for 14% -> 0% of each run, Pallas kernels for 0% -> 0%
where the time goes in v1:
time: 168 us; the launch traced here: 167 us
  Pallas kernels  154 us (92%)
  local copies, waits for them, and re-layouts  7.89 us (5%)
  other arithmetic  4.17 us (2%)
    pallas_call x1, Pallas kernels, body(): pl.pallas_call(functools.partial(m2_kernel, scale), name='m2', out_shape=...  92.3 us
    pallas_call x1, Pallas kernels, body(): pl.pallas_call(m1_kernel, name='m1', out_shape=(sds((4, 4, 2, 4, 16, 2 *...  61.6 us
    unnamed x9, local copies, waits for them, and re-layouts  4.48 us

profile of v1, /device:TPU:0, one launch (start us, length us, event | category | flops | bytes accessed | tf_op | source)
XLA Modules:
  0.0 166.6 jit_solution(2467457077384028123)
XLA Ops:
  0.6 0.7 compare_reduce_fusion
  1.3 1.3 dynamic_slice.3
  2.7 1.2 fusion.11
  3.9 0.6 pad_maximum_fusion.numt_ref
  4.5 0.9 reduce-precision_convert_fusion.1
  5.5 0.7 fusion.5.proj_ref
  6.2 0.0 copy-start.2
  6.2 61.6 %m1.1 = (bf16[4,4,2,4,16,1024]{5,4,3,2,1,0:T(8,128)(2,1)}, bf16[6,1024,256]{2,1,0:T(8,128)(2,1)}, bf16[2,16,512]{2,1,0:T(8,128)(2,1)}, f32[1,512]{1,0:T(1,128)}) custom-call(bf16[48,512]{1,0:T(8,128)(2,1)} %pad_maximum_fusion.numt_ref, bf16[48,2048]{1,0:T(8,128)(2,1)} %fusion.5.proj_ref, bf16[512,2048]{1,0:T(8,128)(2,1)} %bitcast.8, ...), custom_call_target="tpu_custom_call" | custom-call | tf_op jit(solution)/shard_map/m1/pallas_call | solution.py:451
  67.8 0.0 copy-done.2
  67.8 0.7 broadcast_in_dim.14.lev_ref
  68.5 92.3 %m2.1 = (f32[3,16,1024]{2,1,0:T(8,128)}, bf16[512,2048]{1,0:T(8,128)(2,1)}, f32[8,1024]{1,0:T(8,128)}, f32[8,2048]{1,0:T(8,128)}) custom-call(bf16[4,4,2,4,16,1024]{5,4,3,2,1,0:T(8,128)(2,1)} %get-tuple-element.12.xt_ref, bf16[6,1024,256]{2,1,0:T(8,128)(2,1)} %get-tuple-element.13.g_ref, bf16[2,16,512]{2,1,0:T(8,128)(2,1)} %get-tuple-element.14.numt_ref, ...), custom_call_target="tpu_custom_call" | custom-call | tf_op jit(solution)/shard_map/m2/pallas_call | solution.py:476
  160.7 0.0 copy-start
  160.8 0.0 copy-start.1
  160.8 1.4 slice.6
  162.2 3.2 %copy.18 = bf16[1,512,2048]{2,1,0:T(8,128)(2,1)} copy(bf16[1,512,2048]{2,1,0:T(8,128)(2,1)} %bitcast.9) | data formatting | bytes 4194304
  165.3 0.0 copy-done
  165.3 0.7 copy.19
  166.0 0.0 copy-done.1
  166.0 0.6 copy.20
  (1 shorter events, 0.0 us)
Async XLA Ops:
  6.2 61.6 %copy-start.2 = (f32[8]{0:T(128)S(1)}, f32[8]{0:T(128)}, u32[]{:S(2)}) copy-start(f32[8]{0:T(128)} %constant.69) | copy-start | bytes 100
  160.7 4.6 %copy-start = (f32[3,16,1024]{2,1,0:T(8,128)S(1)}, f32[3,16,1024]{2,1,0:T(8,128)}, u32[]{:S(2)}) copy-start(f32[3,16,1024]{2,1,0:T(8,128)} %get-tuple-element.17) | copy-start | bytes 589828
  160.8 5.2 %copy-start.1 = (f32[8,2048]{1,0:T(8,128)S(1)}, f32[8,2048]{1,0:T(8,128)}, u32[]{:S(2)}) copy-start(f32[8,2048]{1,0:T(8,128)} %get-tuple-element.19) | copy-start | bytes 196612

commit v2 on v1

v2 whole, which is shorter than its diff:
```python
import functools
import math

import jax
import jax.numpy as jnp
from jax import lax
from jax.experimental import pallas as pl
from jax.experimental.pallas import tpu as pltpu
from jax.sharding import Mesh
from jax.sharding import PartitionSpec as P

HEADS = 8
DH = 128
T = 512
D = 2048
HALF = 512
ALL = ("z", "y", "c", "x")
MESH = pl.DeviceIdType.MESH
F32 = jnp.float32
BF16 = jnp.bfloat16

fsq_levels = (8, 8, 8, 5, 5, 5)
fsq_bases = (1, 8, 64, 512, 2560, 12800)

NT = (((1,), (1,)), ((), ()))
TN = (((0,), (0,)), ((), ()))


def dot(a, b, dims=None):
    if dims is None:
        return jnp.dot(a, b, preferred_element_type=F32)
    return lax.dot_general(a, b, dims, preferred_element_type=F32)


def entry_barrier(devices):
    barrier = pltpu.get_barrier_semaphore()
    for device in devices:
        pl.semaphore_signal(barrier, inc=1, device_id=device, device_id_type=MESH)
    pl.semaphore_wait(barrier, len(devices))


def send(src, dst, ssem, rsem, device):
    copy = pltpu.make_async_remote_copy(
        src_ref=src, dst_ref=dst, send_sem=ssem, recv_sem=rsem, device_id=device, device_id_type=MESH
    )
    copy.start()
    return copy


def ring(axis, step):
    return lax.rem(lax.axis_index(axis) + step, 4)


PLAN = (("x", 1), ("x", -1), ("y", 1), ("z", 1), ("y", -1), ("z", -1))
ORDER = {"x": ("x", "z", "y"), "y": ("y", "x", "z"), "z": ("z", "y", "x")}
DIMS = {"x": (4, 4, 2), "y": (4, 2, 4), "z": (4, 2, 4)}
DIMS2 = {"x": (4, 2), "y": (4, 2), "z": (2, 4)}


class Trace:
    on = False
    scope = None

    def __call__(self, name=None):
        if not self.on:
            return
        if self.scope is not None:
            self.scope.__exit__(None, None, None)
        self.scope = jax.named_scope(name) if name else None
        if name:
            self.scope.__enter__()


def kernel(
    scale, ids_ref, proj_ref, gain_ref, resid_hbm, og_hbm, wq_hbm, wk_hbm, wv_hbm,
    wout, rg_hbm, gain_out, code_out,
    wbuf, wsem, xb, q, k, v, sqk, dkv, og, ogsem, sc, datt, nf, ns, nall, proj3, gain_row,
    xssem, xrsem, gsem, nsem, free_sem,
    blk, pre, ssend, srecv, s2send, s2recv, sssem, srsem,
    xt_ref, g_ref, igsem, ar, arr, arsem, fs, fr, fsem, rgsem, sems, *scr,
):
    tr = Trace()
    tx, t2 = scr[0:6], scr[6:12]
    recv = [[scr[12 + 18 * phase + 6 * m : 18 + 18 * phase + 6 * m] for m in range(3)] for phase in range(3)]
    c = lax.axis_index("c")
    peer = {"c": 1 - c}
    y = lax.axis_index("y")
    z = lax.axis_index("z")
    own_col = pl.multiple_of(c * HALF, HALF)
    peer_col = pl.multiple_of((1 - c) * HALF, HALF)
    mine = c * 4
    other = (1 - c) * 4

    tr("enter")
    xload = pltpu.make_async_copy(resid_hbm, xb.at[0], ogsem.at[8])
    xload.start()
    loads = []
    for n, w in enumerate((wk_hbm, wv_hbm, wq_hbm)):
        cp = pltpu.make_async_copy(w.at[:, pl.ds(own_col, HALF)], wbuf.at[n], wsem.at[n])
        cp.start()
        loads.append(cp)
    ogloads = []
    for h in range(4):
        for m, (first, col) in enumerate(((other, peer_col), (mine, own_col))):
            cp = pltpu.make_async_copy(
                og_hbm.at[:, pl.ds(pl.multiple_of(col + h * DH, DH), DH)], og.at[first + h], ogsem.at[m * 4 + h])
            cp.start()
            ogloads.append(cp)

    ids = ids_ref[...].astype(F32)
    nf[...] = jnp.zeros_like(nf)
    rest = jnp.zeros((8, D), F32)
    row = lax.broadcasted_iota(jnp.int32, (8, 1), 0)
    inv_level = jnp.zeros((8, 1), F32)
    for j, (level, base) in enumerate(zip(fsq_levels, fsq_bases)):
        quot = jnp.floor((ids + 0.5) * (1.0 / base)) if base > 1 else ids
        digit = quot - level * jnp.floor((quot + 0.5) * (1.0 / level))
        nf[j : j + 1, :] = 2.0 * digit - (level - 1.0)
        inv_level = jnp.where(row == j, 1.0 / (level - 1.0), inv_level)
    proj3[...] = jnp.zeros_like(proj3)
    rest = proj_ref[...] * inv_level[0:6]
    for t in range(3):
        term = rest.astype(BF16)
        proj3[t, 0:6, :] = term
        rest = rest - term.astype(F32)
    nums = nf[...].astype(BF16)
    numt = jnp.concatenate([nums, nums, nums], axis=0)

    barrier_set = [peer] + [{"y": ring("y", s)} for s in (1, 2, 3)] + [{"z": ring("z", s)} for s in (1, 2, 3)]
    entry_barrier(barrier_set + [{"x": ring("x", s)} for s in (1, 3)])

    tr("inputs")
    xload.wait()
    xcopies = []
    for j in range(8):
        cols = slice(j * 256, j * 256 + 256)
        add = dot(numt, proj3[:, :, cols].reshape(48, 256), TN)
        x = (xb[0, :, cols].astype(F32) + add).astype(BF16)
        xb[0, :, cols] = x
        src, dst = tx[2 + j % 4].at[j // 4], recv[0][1 + j // 4][2 + j % 4]
        src[...] = x.astype(F32).reshape(4, 2, 4, 16, 256)
        xcopies.append(send(src, dst, xssem.at[j], xrsem.at[j], peer))
    for h in range(4):
        ogloads[2 * h].wait()
        dkv[h] = og[other + h].astype(F32)
    g_copy = send(dkv.at[0:4], dkv.at[4:8], gsem.at[0], gsem.at[1], peer)
    n_copy = send(nf, ns, nsem.at[0], nsem.at[1], peer)

    def project(slot, n, base):
        for half in range(2):
            p = dot(xb[slot], wbuf[n, :, half * 256 : half * 256 + 256])
            for hh in range(2):
                a = p[:, hh * DH : hh * DH + DH]
                at = base + half * 2 + hh
                if n == 1:
                    v[at] = a.astype(BF16)
                else:
                    s = 1.0 / (1.0 + jnp.exp(-a))
                    slope = s * (1.0 + a * (1.0 - s))
                    if n == 0:
                        k[at] = (a * s).astype(BF16)
                        sqk[8 + at] = slope
                    else:
                        q[at] = (a * s).astype(BF16)
                        sqk[at] = slope

    tr("own_proj")
    for n in range(3):
        loads[n].wait()
        project(0, n, mine)
    for h in range(4):
        ogloads[2 * h + 1].wait()
    tr("peer_wait")
    for j in range(8):
        xcopies[j].wait()
        xb[1, :, j * 256 : j * 256 + 256] = recv[0][1 + j // 4][2 + j % 4][...].reshape(512, 256).astype(BF16)
    tr("peer_kv")
    project(1, 0, other)
    project(1, 1, other)

    def scan_start(s):
        ssend[s, 0] = blk[s, 0, 0:2] + blk[s, 1, 0:2]
        ssend[s, 1] = blk[s, 0, 2:4] + blk[s, 1, 2:4]
        out = []
        for d in (2, 1, 3):
            for half, axis in ((0, "y"), (1, "z")):
                out.append(send(ssend.at[s, half], srecv.at[s, half, d - 1], sssem.at[s, 0, half, d - 1],
                                srsem.at[s, 0, half, d - 1], {axis: ring(axis, d)}))
        return out

    def before(place, d, s):
        return (d <= place) if s == 0 else (d > place)

    def scan_middle(s, sent):
        for cp in sent:
            cp.wait()
        total = ssend[s, 0]
        inside = jnp.zeros_like(total)
        passed = jnp.zeros_like(total)
        for d in (1, 2, 3):
            piece = srecv[s, 0, d - 1]
            total = total + piece
            inside = inside + jnp.where(before(y, d, s), piece, 0.0)
            passed = passed + jnp.where(before(z, d, s), srecv[s, 1, d - 1], 0.0)
        s2send[s, 0] = total
        pre[s, 0:2] = inside
        s2send[s, 1] = passed
        s2send[s, 2] = passed + ssend[s, 1]
        pre[s, 2:4] = passed
        out = []
        for d in (2, 1, 3):
            out.append(send(s2send.at[s, 0], s2recv.at[s, 0, d - 1], sssem.at[s, 1, 0, d - 1],
                            srsem.at[s, 1, 0, d - 1], {"z": ring("z", d)}))
            wraps = (y + d) // 4
            pick = 2 - wraps if s == 0 else 1 + wraps
            out.append(send(s2send.at[s, pick], s2recv.at[s, 1, d - 1], sssem.at[s, 1, 1, d - 1],
                            srsem.at[s, 1, 1, d - 1], {"y": ring("y", d)}))
        return out

    def scan_end(s, sent):
        for cp in sent:
            cp.wait()
        first = pre[s, 0:2]
        second = pre[s, 2:4]
        for d in (1, 2, 3):
            first = first + jnp.where(before(z, d, s), s2recv[s, 0, d - 1], 0.0)
            second = second + s2recv[s, 1, d - 1]
        pre[s, 0:2] = first
        pre[s, 2:4] = second

    def state(s, b, h):
        base = pre[s, h]
        if s == 0:
            return (base + jnp.where(b == 1, blk[0, 0, h], 0.0)).astype(BF16)
        return (base + jnp.where(b == 0, blk[1, 1, h], 0.0)).astype(BF16)

    def kv_step(n, _):
        blk[0, n // 4, lax.rem(n, 4)] = dot(k[n], v[n], TN)
        return 0

    tr("kv")
    lax.fori_loop(0, 8, kv_step, 0)
    sent = scan_start(0)
    tr("qpeer")
    project(1, 2, other)
    g_copy.wait()
    for h in range(4):
        og[other + h] = dkv[4 + h].astype(BF16)
    n_copy.wait()
    nall[c] = nums
    nall[1 - c] = ns[...].astype(BF16)

    row_ids = lax.broadcasted_iota(jnp.int32, (T, T), 0)
    col_ids = lax.broadcasted_iota(jnp.int32, (T, T), 1)

    def score_step(n, _):
        s = jnp.where(col_ids <= row_ids, dot(q[n], k[n], NT), 0.0).astype(BF16)
        sc[n] = s
        dkv[8 + n] = dot(s, v[n])
        return 0

    tr("scores1")
    lax.fori_loop(0, 5, score_step, 0)
    tr("scanmid0")
    sent = scan_middle(0, sent)
    tr("scores2")
    lax.fori_loop(5, 8, score_step, 0)

    def turn_step(n, _):
        cols = pl.ds(pl.multiple_of(n * 128, 128), 128)
        for slot in range(2):
            place = c if slot == 0 else 1 - c
            t = xb[slot, :, cols].T
            xt_ref[n // 4, lax.rem(n, 4), :, :, :, pl.ds(pl.multiple_of(place * T, T), T)] = t.reshape(2, 4, 16, T)
        return 0

    tr("turn")
    lax.fori_loop(0, 16, turn_step, 0)
    tr("scanend0")
    scan_end(0, sent)

    def forward_step(n, _):
        b = n // 4
        h = lax.rem(n, 4)
        a = dkv[8 + n] + dot(q[n], state(0, b, h))
        root = jnp.sqrt(jnp.mean(a * a, axis=-1, keepdims=True) + 1e-06)
        inv = 1.0 / root
        normed = a * inv
        g = og[n].astype(F32)
        dn = g * gain_ref[:, pl.ds(pl.multiple_of(c * HALF + h * DH, DH), DH)]
        da = ((dn - normed * jnp.mean(dn * normed, axis=-1, keepdims=True)) * inv).astype(BF16)
        datt[n] = da
        gain_row[n] = jnp.sum(g * normed, axis=0, keepdims=True)
        blk[1, b, h] = dot(q[n], da, TN)
        return 0

    tr("fwd")
    lax.fori_loop(0, 8, forward_step, 0)
    sent = scan_start(1)

    def put(kind, n, value):
        b = n // 4
        h = lax.rem(n, 4)
        g_ref[kind * 2 + h // 2, pl.ds(pl.multiple_of(b * T, T), T),
              pl.ds(pl.multiple_of(lax.rem(h, 2) * DH, DH), DH)] = value.astype(BF16)

    def back_step(n, _):
        b = n // 4
        h = lax.rem(n, 4)
        da = datt[n]
        bs = jnp.where(col_ids <= row_ids, dot(da, v[n], NT), 0.0).astype(BF16)
        dq = dot(bs, k[n]) + dot(da, state(0, b, h), NT)
        put(0, n, dq * sqk[n])
        dkv[n] = dot(bs, q[n], TN)
        dkv[8 + n] = dot(sc[n], da, TN)
        return 0

    def lhs(axis, i):
        if axis == "x":
            rows = xt_ref[:, :, :, i]
        elif axis == "y":
            rows = xt_ref[:, i]
        else:
            rows = xt_ref[i]
        return rows.reshape(512, 1024)

    def product(hp, i):
        axis = PLAN[hp][0]
        return dot(lhs(axis, i), g_ref[hp]).reshape(*DIMS[axis], 16, 256)

    sends = {}

    def go(hp, phase, m, src, dirn):
        axis = ORDER[PLAN[hp][0]][phase]
        sends[hp, phase, m] = send(src, recv[phase][m][hp], sems.at[0, hp, phase, m], sems.at[1, hp, phase, m],
                                   {axis: ring(axis, 1 if dirn == 1 else 3)})

    def far(hps):
        for hp in hps:
            tx[hp][0] = product(hp, ring(PLAN[hp][0], 2))
        for hp in hps:
            go(hp, 0, 0, tx[hp].at[0], PLAN[hp][1])

    def straight(hps):
        for hp in hps:
            axis, d = PLAN[hp]
            tx[hp][1] = product(hp, ring(axis, 3 if d == 1 else 1))
        for hp in hps:
            go(hp, 0, 1, tx[hp].at[1], -PLAN[hp][1])

    tr("back1")
    lax.fori_loop(0, 5, back_step, 0)
    tr("scanmid1")
    sent = scan_middle(1, sent)
    tr("back2")
    lax.fori_loop(5, 8, back_step, 0)
    tr("xfirst")
    far((0, 1))
    straight((0, 1))
    tr("scanend1")
    scan_end(1, sent)

    def last_step(n, _):
        st = state(1, n // 4, lax.rem(n, 4))
        put(1, n, (dkv[n] + dot(v[n], st, NT)) * sqk[8 + n])
        put(2, n, dkv[8 + n] + dot(k[n], st))
        return 0

    tr("last")
    lax.fori_loop(0, 8, last_step, 0)
    pl.semaphore_signal(free_sem, inc=1, device_id=peer, device_id_type=MESH)
    tr("yzfirst")
    far((2, 3))
    far((4, 5))
    straight((2, 3, 4, 5))

    tr("small")
    smalls = []
    for t in range(3):
        parts = []
        for hp in (2 * t, 2 * t + 1):
            s = dot(nall[0], g_ref[hp, 0:T, :]) + dot(nall[1], g_ref[hp, T : 2 * T, :])
            s = s[0:8] * inv_level
            terms = []
            for _ in range(3):
                term = s.astype(BF16).astype(F32)
                s = s - term
                terms.append(term)
            terms.append(jnp.zeros_like(s))
            parts.append(jnp.concatenate(terms, axis=0))
        smalls.append(jnp.concatenate(parts, axis=1).astype(BF16))

    order_w = (2, 0, 1)

    def ig_tile(n, base, extra):
        total = None
        rows = pl.ds(pl.multiple_of(base, T), T)
        for t in range(3):
            left = jnp.concatenate([g_ref[2 * t, rows, :], g_ref[2 * t + 1, rows, :]], axis=1)
            if extra:
                left = jnp.concatenate([left, smalls[t]], axis=0)
            part = dot(left, wbuf[order_w[t], pl.ds(pl.multiple_of(n * 256, 256), 256), :], NT)
            total = part if total is None else total + part
        return total

    def ig_peer(n, _):
        total = ig_tile(n, (1 - c) * T, True)
        dkv[2 * n] = total[0:T, 0:DH]
        dkv[2 * n + 1] = total[0:T, DH : 2 * DH]
        code = total[T : T + 8] + total[T + 8 : T + 16] + total[T + 16 : T + 24]
        ar[0, :, pl.ds(pl.multiple_of(n * 256, 256), 256)] = code
        return 0

    tr("ig1")
    lax.fori_loop(0, 8, ig_peer, 0)
    ar[0, 6:7, :] = jnp.zeros((1, D), F32)
    for h in range(4):
        ar[0, 6:7, pl.ds(pl.multiple_of(c * HALF + h * DH, DH), DH)] = gain_row[h] + gain_row[4 + h]

    steps = [("c", 0)] + [(a, m) for a in ("x", "y", "z") for m in (0, 1)]

    def small(n):
        axis, m = steps[n]
        i = lax.axis_index(axis)
        partner = 3 - i if m else i + 1 - 2 * lax.rem(i, 2)
        return send(ar.at[n], arr.at[n], arsem.at[0, n], arsem.at[1, n], {axis: partner})

    def small_next(n, cp):
        cp.wait()
        ar[n + 1] = ar[n] + arr[n]
        return small(n + 1) if n + 1 < 7 else None

    small_copy = small(0)
    pl.semaphore_wait(free_sem, 1)
    ig_copy = send(dkv, sqk, igsem.at[0], igsem.at[1], peer)

    def relay(hp):
        axis, d = PLAN[hp]
        mid = product(hp, ring(axis, 1 if d == 1 else 3))
        sends[hp, 0, 0].wait_recv()
        recv[0][0][hp][...] = recv[0][0][hp][...] + mid
        go(hp, 0, 2, recv[0][0][hp], d)

    tr("relay")
    small_copy = small_next(0, small_copy)
    for hp in (0, 1, 2, 3, 4, 5):
        relay(hp)
    tr("own")
    for hp in range(6):
        sends[hp, 0, 0].wait_send()
    for hp in range(6):
        tx[hp][0] = product(hp, ring(PLAN[hp][0], 0))

    tr("ig2")
    ig_copy.wait()

    def ig_own(n, _):
        total = ig_tile(n, c * T, False)
        total = total + jnp.concatenate([sqk[2 * n], sqk[2 * n + 1]], axis=1)
        xb[0, :, pl.ds(pl.multiple_of(n * 256, 256), 256)] = total.astype(BF16)
        return 0

    lax.fori_loop(0, 8, ig_own, 0)
    rg_copy = pltpu.make_async_copy(xb.at[0], rg_hbm, rgsem)
    rg_copy.start()

    def piece(hp, phase, i):
        axis = PLAN[hp][0]
        if phase == 1:
            return tx[hp].at[0, :, :, i] if axis == "y" else tx[hp].at[0, i]
        return t2[hp].at[:, i] if axis == "z" else t2[hp].at[i]

    order = (0, 1, 2, 3, 4, 5)
    stage = 1
    for phase in (1, 2):
        tr("ph%da" % phase)
        for hp in order:
            axis, d = ORDER[PLAN[hp][0]][phase], PLAN[hp][1]
            sends[hp, phase - 1, 1].wait_recv()
            sends[hp, phase - 1, 2].wait_recv()
            arrived = recv[phase - 1][1][hp][...] + recv[phase - 1][2][hp][...]
            if phase == 1:
                tx[hp][0] = tx[hp][0] + arrived
            else:
                t2[hp][...] = piece(hp, 1, ring(ORDER[PLAN[hp][0]][1], 0))[...] + arrived
            go(hp, phase, 0, piece(hp, phase, ring(axis, 2)), d)
            go(hp, phase, 1, piece(hp, phase, ring(axis, 3 if d == 1 else 1)), -d)
        small_copy = small_next(stage, small_copy)
        stage += 1
        tr("ph%db" % phase)
        for hp in order:
            axis, d = ORDER[PLAN[hp][0]][phase], PLAN[hp][1]
            sends[hp, phase, 0].wait_recv()
            via = recv[phase][0][hp]
            via[...] = via[...] + piece(hp, phase, ring(axis, 1 if d == 1 else 3))[...]
            go(hp, phase, 2, via, d)
        small_copy = small_next(stage, small_copy)
        stage += 1

    tr("final")
    for hp in range(6):
        sends[hp, 2, 1].wait_recv()
        sends[hp, 2, 2].wait_recv()
        last = ORDER[PLAN[hp][0]][2]
        fs[:, :, hp * 256 : hp * 256 + 256] = (
            piece(hp, 2, ring(last, 0))[...] + recv[2][1][hp][...] + recv[2][2][hp][...]
        ) * scale
    f_copy = send(fs.at[1 - c], fr, fsem.at[0], fsem.at[1], peer)
    for t in range(3):
        wout[t, :, pl.ds(own_col, HALF)] = fs[c, :, t * HALF : t * HALF + HALF]
    while stage < 7:
        small_copy = small_next(stage, small_copy)
        stage += 1
    code_out[...] = ar[7, 0:6, :] * scale
    gain_out[...] = ar[7, 6:7, 0 : 2 * HALF] * scale
    f_copy.wait()
    for t in range(3):
        wout[t, :, pl.ds(peer_col, HALF)] = fr[:, t * HALF : t * HALF + HALF]
    tr("drain")
    for (hp, phase, m), cp in sends.items():
        if (phase, m) != (0, 0):
            cp.wait_send()
    rg_copy.wait()
    tr()


def vmem(*shape, dtype=F32):
    return pltpu.VMEM(shape, dtype)


def body(resid, token_ids, code_proj, w_query, w_key, w_value, gain, out_grad):
    dma = pltpu.SemaphoreType.DMA
    any_spec = pl.BlockSpec(memory_space=pl.ANY)
    vm = pl.BlockSpec(memory_space=pltpu.VMEM)
    sds = jax.ShapeDtypeStruct
    scale = 1.0 / math.sqrt(T * lax.axis_size(ALL))
    w_out, resid_grad, gain_out, code_out = pl.pallas_call(
        functools.partial(kernel, scale),
        name="layer",
        out_shape=(sds((3, 16, 2 * HALF), F32), sds((T, D), BF16), sds((1, 2 * HALF), F32), sds((6, D), F32)),
        in_specs=[vm] * 3 + [any_spec] * 5,
        out_specs=(vm, any_spec, vm, vm),
        scratch_shapes=[
            vmem(3, D, HALF, dtype=BF16), dma((3,)), vmem(2, T, D, dtype=BF16),
            vmem(8, T, DH, dtype=BF16), vmem(8, T, DH, dtype=BF16), vmem(8, T, DH, dtype=BF16),
            vmem(16, T, DH), vmem(16, T, DH), vmem(8, T, DH, dtype=BF16), dma((9,)),
            vmem(8, T, T, dtype=BF16), vmem(8, T, DH, dtype=BF16),
            vmem(16, T), vmem(16, T), vmem(2, 16, T, dtype=BF16), vmem(3, 16, D, dtype=BF16), vmem(8, 1, DH),
            dma((8,)), dma((8,)), dma((2,)), dma((2,)), pltpu.SemaphoreType.REGULAR,
            vmem(2, 2, 4, DH, DH), vmem(2, 4, DH, DH),
            vmem(2, 2, 2, DH, DH), vmem(2, 2, 3, 2, DH, DH), vmem(2, 3, 2, DH, DH), vmem(2, 2, 3, 2, DH, DH),
            dma((2, 2, 2, 3)), dma((2, 2, 2, 3)),
            vmem(4, 4, 2, 4, 16, 2 * T, dtype=BF16), vmem(6, 2 * T, 256, dtype=BF16), dma((2,)),
            vmem(8, 8, D), vmem(7, 8, D), dma((2, 7)),
            vmem(2, 16, 3 * HALF), vmem(16, 3 * HALF), dma((2,)), dma,
            dma((2, 6, 3, 3)),
            *[vmem(2, *DIMS[a], 16, 256) for a, _ in PLAN],
            *[vmem(*DIMS2[a], 16, 256) for a, _ in PLAN],
            *[vmem(*DIMS[a], 16, 256) for _ in range(3) for a, _ in PLAN],
            *[vmem(*DIMS2[a], 16, 256) for _ in range(3) for a, _ in PLAN],
            *[vmem(2, 16, 256) for _ in range(3) for a, _ in PLAN],
        ],
        compiler_params=pltpu.CompilerParams(collective_id=0, has_side_effects=True, vmem_limit_bytes=67_043_328),
    )(token_ids, code_proj, gain[None], resid[0], out_grad[0], w_query, w_key, w_value)
    return resid_grad[None], w_out.transpose(1, 0, 2), gain_out[0], code_out


def solution(mesh):
    finer = Mesh(mesh.devices.reshape(4, 4, 2, 4), ALL)
    seq = ("z", "y", "c")
    return jax.shard_map(
        body,
        mesh=finer,
        in_specs=(P("x", seq, None), P("x", seq), P(), P(), P(), P(), P(), P("x", seq, None)),
        out_specs=(P("x", seq, None), P(ALL, None, None), P(), P()),
        check_vma=False,
    )
```

time: 168 us -> 127 us (0.76)
  Pallas kernels: 154 us -> 121 us
  other arithmetic: 4.17 us -> 0 us
  local copies, waits for them, and re-layouts: 7.89 us -> 5.11 us
    pallas_call x2 -> x1, Pallas kernels: 154 us -> 121 us  [body(): pl.pallas_call(functools.partial(kernel, scale), name='layer', out_shape=...]
    convert_element_type x2 -> x0, other arithmetic: 2.14 us -> none  [the longest x1 1.22 us: body(): nums = (2 * (token_ids // bases % levels) - (levels - 1)).astype(BF16)]
    unnamed x9 -> x10, local copies, waits for them, and re-layouts: 4.48 us -> 5.11 us
where the time goes in v2:
time: 127 us
  Pallas kernels  121 us (95%)
  local copies, waits for them, and re-layouts  5.11 us (4%)
    pallas_call x1, Pallas kernels, body(): pl.pallas_call(functools.partial(kernel, scale), name='layer', out_shape=...  121 us
    unnamed x10, local copies, waits for them, and re-layouts  5.11 us

profile of v2, /device:TPU:0, one launch (start us, length us, event | category | flops | bytes accessed | tf_op | source)
XLA Modules:
  0.0 126.9 jit_solution(9310719995700193105)
XLA Ops:
  0.6 121.1 %layer.1 = (f32[3,16,1024]{2,1,0:T(8,128)}, bf16[512,2048]{1,0:T(8,128)(2,1)}, f32[1,1024]{1,0:T(1,128)}, f32[6,2048]{1,0:T(8,128)}) custom-call(s32[1,512]{1,0:T(1,128)} %ids_ref.1, f32[6,2048]{1,0:T(8,128)} %proj_ref.1, f32[1,1024]{1,0:T(1,128)} %bitcast.10, bf16[512,2048]{1,0:T(8,128)(2,1)} %bitcast.6, bf16[512,1024]{1,0:T(8,128)(2,1)} %bitcast.8, ...), custom_call_target="tpu_custom_call" | custom-call | tf_op jit(solution)/shard_map/layer/pallas_call | solution.py:537
  121.7 0.0 copy-start
  121.7 0.0 copy-start.2
  121.7 0.0 copy-start.1
  121.8 3.2 %copy.16 = bf16[1,512,2048]{2,1,0:T(8,128)(2,1)} copy(bf16[1,512,2048]{2,1,0:T(8,128)(2,1)} %bitcast.7) | data formatting | bytes 4194304
  125.0 0.0 copy-done
  125.0 0.7 copy.17
  125.6 0.0 copy-done.2
  125.6 0.6 copy.18
  126.2 0.0 copy-done.1
  126.2 0.6 copy.19
Async XLA Ops:
  121.7 3.2 %copy-start = (f32[3,16,1024]{2,1,0:T(8,128)S(1)}, f32[3,16,1024]{2,1,0:T(8,128)}, u32[]{:S(2)}) copy-start(f32[3,16,1024]{2,1,0:T(8,128)} %get-tuple-element.9) | copy-start | bytes 589828
  121.7 3.9 %copy-start.2 = (f32[1,1024]{1,0:T(1,128)S(1)}, f32[1,1024]{1,0:T(1,128)}, u32[]{:S(2)}) copy-start(f32[1,1024]{1,0:T(1,128)} %get-tuple-element.10) | copy-start | bytes 12292
  121.7 4.5 %copy-start.1 = (f32[6,2048]{1,0:T(8,128)S(1)}, f32[6,2048]{1,0:T(8,128)}, u32[]{:S(2)}) copy-start(f32[6,2048]{1,0:T(8,128)} %get-tuple-element.19) | copy-start | bytes 147460

commit v3 on v2

--- a/solution.py
+++ b/solution.py
@@ -76,10 +76,19 @@
     wout, rg_hbm, gain_out, code_out,
     wbuf, wsem, xb, q, k, v, sqk, dkv, og, ogsem, sc, datt, nf, ns, nall, proj3, gain_row,
     xssem, xrsem, gsem, nsem, free_sem,
-    blk, pre, ssend, srecv, s2send, s2recv, sssem, srsem,
+    blk, pre, sbuf, rbuf, obuf, sssem, srsem,
     xt_ref, g_ref, igsem, ar, arr, arsem, fs, fr, fsem, rgsem, sems, *scr,
 ):
     tr = Trace()
+
+    def pairs(first, last, step):
+        def two(i, _):
+            step(2 * i)
+            step(2 * i + 1)
+            return 0
+
+        lax.fori_loop(first // 2, last // 2, two, 0)
+
     tx, t2 = scr[0:6], scr[6:12]
     recv = [[scr[12 + 18 * phase + 6 * m : 18 + 18 * phase + 6 * m] for m in range(3)] for phase in range(3)]
     c = lax.axis_index("c")
@@ -126,8 +135,8 @@
     nums = nf[...].astype(BF16)
     numt = jnp.concatenate([nums, nums, nums], axis=0)
 
-    barrier_set = [peer] + [{"y": ring("y", s)} for s in (1, 2, 3)] + [{"z": ring("z", s)} for s in (1, 2, 3)]
-    entry_barrier(barrier_set + [{"x": ring("x", s)} for s in (1, 3)])
+    plane = [{"z": ring("z", dz), "y": ring("y", dy)} for dz in range(4) for dy in range(4) if dz or dy]
+    entry_barrier([peer] + plane + [{"x": ring("x", n)} for n in (1, 2, 3)])
 
     tr("inputs")
     xload.wait()
@@ -164,10 +173,18 @@
                         q[at] = (a * s).astype(BF16)
                         sqk[at] = slope
 
+    def kv_step(n):
+        blk[0, n // 4, lax.rem(n, 4)] = dot(k[n], v[n], TN)
+
+    def kv_steps(base):
+        for h in range(4):
+            kv_step(base + h)
+
     tr("own_proj")
-    for n in range(3):
+    for n in range(2):
         loads[n].wait()
         project(0, n, mine)
+    kv_steps(mine)
     for h in range(4):
         ogloads[2 * h + 1].wait()
     tr("peer_wait")
@@ -178,70 +195,50 @@
     project(1, 0, other)
     project(1, 1, other)
 
+    me = z * 4 + y
+    spots = sorted(((dz, dy) for dz in range(4) for dy in range(4) if dz or dy),
+                   key=lambda o: -(min(o[0], 4 - o[0]) + min(o[1], 4 - o[1])))
+
+    def to_all(src, dst, n):
+        out = []
+        for o, (dz, dy) in enumerate(spots):
+            zt, yt = ring("z", dz), ring("y", dy)
+            out.append(send(src.at[zt * 4 + yt], dst.at[me], sssem.at[n, o], srsem.at[n, o], {"z": zt, "y": yt}))
+        return out
+
     def scan_start(s):
-        ssend[s, 0] = blk[s, 0, 0:2] + blk[s, 1, 0:2]
-        ssend[s, 1] = blk[s, 0, 2:4] + blk[s, 1, 2:4]
-        out = []
-        for d in (2, 1, 3):
-            for half, axis in ((0, "y"), (1, "z")):
-                out.append(send(ssend.at[s, half], srecv.at[s, half, d - 1], sssem.at[s, 0, half, d - 1],
-                                srsem.at[s, 0, half, d - 1], {axis: ring(axis, d)}))
+        sbuf[s] = (blk[s, 0] + blk[s, 1]).reshape(16, 32, DH)
+        out = to_all(sbuf.at[s], rbuf.at[s], 2 * s)
+        rbuf[s, me] = sbuf[s, me]
         return out
-
-    def before(place, d, s):
-        return (d <= place) if s == 0 else (d > place)
 
     def scan_middle(s, sent):
         for cp in sent:
             cp.wait()
-        total = ssend[s, 0]
-        inside = jnp.zeros_like(total)
-        passed = jnp.zeros_like(total)
-        for d in (1, 2, 3):
-            piece = srecv[s, 0, d - 1]
-            total = total + piece
-            inside = inside + jnp.where(before(y, d, s), piece, 0.0)
-            passed = passed + jnp.where(before(z, d, s), srecv[s, 1, d - 1], 0.0)
-        s2send[s, 0] = total
-        pre[s, 0:2] = inside
-        s2send[s, 1] = passed
-        s2send[s, 2] = passed + ssend[s, 1]
-        pre[s, 2:4] = passed
-        out = []
-        for d in (2, 1, 3):
-            out.append(send(s2send.at[s, 0], s2recv.at[s, 0, d - 1], sssem.at[s, 1, 0, d - 1],
-                            srsem.at[s, 1, 0, d - 1], {"z": ring("z", d)}))
-            wraps = (y + d) // 4
-            pick = 2 - wraps if s == 0 else 1 + wraps
-            out.append(send(s2send.at[s, pick], s2recv.at[s, 1, d - 1], sssem.at[s, 1, 1, d - 1],
-                            srsem.at[s, 1, 1, d - 1], {"y": ring("y", d)}))
+        total = jnp.zeros((32, DH), F32)
+        for i in range(16) if s == 0 else reversed(range(16)):
+            obuf[s, i] = total
+            total = total + rbuf[s, i]
+        out = to_all(obuf.at[s], pre.at[s], 2 * s + 1)
+        pre[s, me] = obuf[s, me]
         return out
 
     def scan_end(s, sent):
         for cp in sent:
             cp.wait()
-        first = pre[s, 0:2]
-        second = pre[s, 2:4]
-        for d in (1, 2, 3):
-            first = first + jnp.where(before(z, d, s), s2recv[s, 0, d - 1], 0.0)
-            second = second + s2recv[s, 1, d - 1]
-        pre[s, 0:2] = first
-        pre[s, 2:4] = second
 
     def state(s, b, h):
-        base = pre[s, h]
+        base = pre[s, pl.ds(4 * h, 4)].reshape(DH, DH)
         if s == 0:
             return (base + jnp.where(b == 1, blk[0, 0, h], 0.0)).astype(BF16)
         return (base + jnp.where(b == 0, blk[1, 1, h], 0.0)).astype(BF16)
 
-    def kv_step(n, _):
-        blk[0, n // 4, lax.rem(n, 4)] = dot(k[n], v[n], TN)
-        return 0
-
     tr("kv")
-    lax.fori_loop(0, 8, kv_step, 0)
+    kv_steps(other)
     sent = scan_start(0)
-    tr("qpeer")
+    tr("qproj")
+    loads[2].wait()
+    project(0, 2, mine)
     project(1, 2, other)
     g_copy.wait()
     for h in range(4):
@@ -253,33 +250,31 @@
     row_ids = lax.broadcasted_iota(jnp.int32, (T, T), 0)
     col_ids = lax.broadcasted_iota(jnp.int32, (T, T), 1)
 
-    def score_step(n, _):
+    def score_step(n):
         s = jnp.where(col_ids <= row_ids, dot(q[n], k[n], NT), 0.0).astype(BF16)
         sc[n] = s
         dkv[8 + n] = dot(s, v[n])
-        return 0
 
     tr("scores1")
-    lax.fori_loop(0, 5, score_step, 0)
+    pairs(0, 4, score_step)
     tr("scanmid0")
     sent = scan_middle(0, sent)
     tr("scores2")
-    lax.fori_loop(5, 8, score_step, 0)
-
-    def turn_step(n, _):
+    pairs(4, 8, score_step)
+
+    def turn_step(n):
         cols = pl.ds(pl.multiple_of(n * 128, 128), 128)
         for slot in range(2):
             place = c if slot == 0 else 1 - c
             t = xb[slot, :, cols].T
             xt_ref[n // 4, lax.rem(n, 4), :, :, :, pl.ds(pl.multiple_of(place * T, T), T)] = t.reshape(2, 4, 16, T)
-        return 0
 
     tr("turn")
-    lax.fori_loop(0, 16, turn_step, 0)
+    pairs(0, 16, turn_step)
     tr("scanend0")
     scan_end(0, sent)
 
-    def forward_step(n, _):
+    def forward_step(n):
         b = n // 4
         h = lax.rem(n, 4)
         a = dkv[8 + n] + dot(q[n], state(0, b, h))
@@ -292,10 +287,9 @@
         datt[n] = da
         gain_row[n] = jnp.sum(g * normed, axis=0, keepdims=True)
         blk[1, b, h] = dot(q[n], da, TN)
-        return 0
 
     tr("fwd")
-    lax.fori_loop(0, 8, forward_step, 0)
+    pairs(0, 8, forward_step)
     sent = scan_start(1)
 
     def put(kind, n, value):
@@ -304,7 +298,7 @@
         g_ref[kind * 2 + h // 2, pl.ds(pl.multiple_of(b * T, T), T),
               pl.ds(pl.multiple_of(lax.rem(h, 2) * DH, DH), DH)] = value.astype(BF16)
 
-    def back_step(n, _):
+    def back_step(n):
         b = n // 4
         h = lax.rem(n, 4)
         da = datt[n]
@@ -313,7 +307,6 @@
         put(0, n, dq * sqk[n])
         dkv[n] = dot(bs, q[n], TN)
         dkv[8 + n] = dot(sc[n], da, TN)
-        return 0
 
     def lhs(axis, i):
         if axis == "x":
@@ -349,25 +342,24 @@
             go(hp, 0, 1, tx[hp].at[1], -PLAN[hp][1])
 
     tr("back1")
-    lax.fori_loop(0, 5, back_step, 0)
+    pairs(0, 4, back_step)
     tr("scanmid1")
     sent = scan_middle(1, sent)
     tr("back2")
-    lax.fori_loop(5, 8, back_step, 0)
+    pairs(4, 8, back_step)
     tr("xfirst")
     far((0, 1))
     straight((0, 1))
     tr("scanend1")
     scan_end(1, sent)
 
-    def last_step(n, _):
+    def last_step(n):
         st = state(1, n // 4, lax.rem(n, 4))
         put(1, n, (dkv[n] + dot(v[n], st, NT)) * sqk[8 + n])
         put(2, n, dkv[8 + n] + dot(k[n], st))
-        return 0
 
     tr("last")
-    lax.fori_loop(0, 8, last_step, 0)
+    pairs(0, 8, last_step)
     pl.semaphore_signal(free_sem, inc=1, device_id=peer, device_id_type=MESH)
     tr("yzfirst")
     far((2, 3))
@@ -452,6 +444,7 @@
         tx[hp][0] = product(hp, ring(PLAN[hp][0], 0))
 
     tr("ig2")
+    small_copy = small_next(1, small_copy)
     ig_copy.wait()
 
     def ig_own(n, _):
@@ -470,47 +463,49 @@
             return tx[hp].at[0, :, :, i] if axis == "y" else tx[hp].at[0, i]
         return t2[hp].at[:, i] if axis == "z" else t2[hp].at[i]
 
-    order = (0, 1, 2, 3, 4, 5)
-    stage = 1
-    for phase in (1, 2):
-        tr("ph%da" % phase)
-        for hp in order:
-            axis, d = ORDER[PLAN[hp][0]][phase], PLAN[hp][1]
-            sends[hp, phase - 1, 1].wait_recv()
-            sends[hp, phase - 1, 2].wait_recv()
-            arrived = recv[phase - 1][1][hp][...] + recv[phase - 1][2][hp][...]
-            if phase == 1:
-                tx[hp][0] = tx[hp][0] + arrived
-            else:
-                t2[hp][...] = piece(hp, 1, ring(ORDER[PLAN[hp][0]][1], 0))[...] + arrived
-            go(hp, phase, 0, piece(hp, phase, ring(axis, 2)), d)
-            go(hp, phase, 1, piece(hp, phase, ring(axis, 3 if d == 1 else 1)), -d)
-        small_copy = small_next(stage, small_copy)
-        stage += 1
-        tr("ph%db" % phase)
-        for hp in order:
-            axis, d = ORDER[PLAN[hp][0]][phase], PLAN[hp][1]
-            sends[hp, phase, 0].wait_recv()
-            via = recv[phase][0][hp]
-            via[...] = via[...] + piece(hp, phase, ring(axis, 1 if d == 1 else 3))[...]
-            go(hp, phase, 2, via, d)
-        small_copy = small_next(stage, small_copy)
-        stage += 1
+    def ends(hp, phase):
+        sends[hp, phase, 1].wait_recv()
+        sends[hp, phase, 2].wait_recv()
+        return recv[phase][1][hp][...] + recv[phase][2][hp][...]
+
+    tr("ph1a")
+    for hp in range(6):
+        axis, d = ORDER[PLAN[hp][0]][1], PLAN[hp][1]
+        tx[hp][0] = tx[hp][0] + ends(hp, 0)
+        go(hp, 1, 0, piece(hp, 1, ring(axis, 2)), d)
+        go(hp, 1, 1, piece(hp, 1, ring(axis, 3 if d == 1 else 1)), -d)
+        if hp == 1:
+            small_copy = small_next(2, small_copy)
+    tr("ph1b")
+    for hp in range(6):
+        axis, d = ORDER[PLAN[hp][0]][1], PLAN[hp][1]
+        sends[hp, 1, 0].wait_recv()
+        via = recv[1][0][hp]
+        via[...] = via[...] + piece(hp, 1, ring(axis, 1 if d == 1 else 3))[...]
+        go(hp, 1, 2, via, d)
+        if hp == 1:
+            small_copy = small_next(3, small_copy)
+    small_copy = small_next(4, small_copy)
+    tr("ph2a")
+    for hp in range(6):
+        before, axis = ORDER[PLAN[hp][0]][1:]
+        t2[hp][...] = piece(hp, 1, ring(before, 0))[...] + ends(hp, 1)
+        for m in range(3):
+            sends[hp, 2, m] = send(piece(hp, 2, ring(axis, m + 1)), recv[2][m][hp], sems.at[0, hp, 2, m],
+                                   sems.at[1, hp, 2, m], {axis: ring(axis, m + 1)})
+    small_copy = small_next(5, small_copy)
 
     tr("final")
     for hp in range(6):
-        sends[hp, 2, 1].wait_recv()
-        sends[hp, 2, 2].wait_recv()
+        sends[hp, 2, 0].wait_recv()
         last = ORDER[PLAN[hp][0]][2]
         fs[:, :, hp * 256 : hp * 256 + 256] = (
-            piece(hp, 2, ring(last, 0))[...] + recv[2][1][hp][...] + recv[2][2][hp][...]
+            piece(hp, 2, ring(last, 0))[...] + recv[2][0][hp][...] + ends(hp, 2)
         ) * scale
     f_copy = send(fs.at[1 - c], fr, fsem.at[0], fsem.at[1], peer)
     for t in range(3):
         wout[t, :, pl.ds(own_col, HALF)] = fs[c, :, t * HALF : t * HALF + HALF]
-    while stage < 7:
-        small_copy = small_next(stage, small_copy)
-        stage += 1
+    small_next(6, small_copy)
     code_out[...] = ar[7, 0:6, :] * scale
     gain_out[...] = ar[7, 6:7, 0 : 2 * HALF] * scale
     f_copy.wait()
@@ -522,6 +517,11 @@
             cp.wait_send()
     rg_copy.wait()
     tr()
+
+
+def hand_over(*refs):
+    for n in range(4):
+        refs[4 + n][...] = refs[n][...]
 
 
 def vmem(*shape, dtype=F32):
@@ -547,9 +547,8 @@
             vmem(8, T, T, dtype=BF16), vmem(8, T, DH, dtype=BF16),
             vmem(16, T), vmem(16, T), vmem(2, 16, T, dtype=BF16), vmem(3, 16, D, dtype=BF16), vmem(8, 1, DH),
             dma((8,)), dma((8,)), dma((2,)), dma((2,)), pltpu.SemaphoreType.REGULAR,
-            vmem(2, 2, 4, DH, DH), vmem(2, 4, DH, DH),
-            vmem(2, 2, 2, DH, DH), vmem(2, 2, 3, 2, DH, DH), vmem(2, 3, 2, DH, DH), vmem(2, 2, 3, 2, DH, DH),
-            dma((2, 2, 2, 3)), dma((2, 2, 2, 3)),
+            vmem(2, 2, 4, DH, DH), vmem(2, 16, 32, DH), vmem(2, 16, 32, DH), vmem(2, 16, 32, DH), vmem(2, 16, 32, DH),
+            dma((4, 15)), dma((4, 15)),
             vmem(4, 4, 2, 4, 16, 2 * T, dtype=BF16), vmem(6, 2 * T, 256, dtype=BF16), dma((2,)),
             vmem(8, 8, D), vmem(7, 8, D), dma((2, 7)),
             vmem(2, 16, 3 * HALF), vmem(16, 3 * HALF), dma((2,)), dma,
@@ -562,6 +561,17 @@
         ],
         compiler_params=pltpu.CompilerParams(collective_id=0, has_side_effects=True, vmem_limit_bytes=67_043_328),
     )(token_ids, code_proj, gain[None], resid[0], out_grad[0], w_query, w_key, w_value)
+    rows = T // 4
+    block = pl.BlockSpec((rows, D), lambda i: (i, 0))
+    whole = [pl.BlockSpec(shape, lambda i, n=len(shape): (0,) * n) for shape in ((3, 16, 2 * HALF), (1, 2 * HALF), (6, D))]
+    resid_grad, w_out, gain_out, code_out = pl.pallas_call(
+        hand_over,
+        name="hand_over",
+        grid=(4,),
+        out_shape=(sds((T, D), BF16), sds((3, 16, 2 * HALF), F32), sds((1, 2 * HALF), F32), sds((6, D), F32)),
+        in_specs=[block] + whole,
+        out_specs=(block, *whole),
+    )(resid_grad, w_out, gain_out, code_out)
     return resid_grad[None], w_out.transpose(1, 0, 2), gain_out[0], code_out
 
 

time: 127 us -> 110 us (0.87)
  Pallas kernels: 121 us -> 108 us
  local copies, waits for them, and re-layouts: 5.11 us -> 0 us
    pallas_call x1, Pallas kernels: 121 us -> 104 us  [body(): pl.pallas_call(functools.partial(kernel, scale), name='layer', out_shape=...]
    unnamed x10 -> x0, local copies, waits for them, and re-layouts: 5.11 us -> none
    pallas_call x0 -> x1, Pallas kernels: none -> 3.92 us  [body(): pl.pallas_call(hand_over, name='hand_over', grid=(4,), out_shape=(sds((T,...]
where the time goes in v3:
time: 110 us; the launch traced here: 109 us
  Pallas kernels  108 us (98%)
    pallas_call x1, Pallas kernels, body(): pl.pallas_call(functools.partial(kernel, scale), name='layer', out_shape=...  104 us
    pallas_call x1, Pallas kernels, body(): pl.pallas_call(hand_over, name='hand_over', grid=(4,), out_shape=(sds((T,...  3.92 us

profile of v3, /device:TPU:0, one launch (start us, length us, event | category | flops | bytes accessed | tf_op | source)
XLA Modules:
  0.0 109.0 jit_solution(16193605574379507539)
XLA Ops:
  0.6 104.4 %layer.1 = (f32[3,16,1024]{2,1,0:T(8,128)}, bf16[512,2048]{1,0:T(8,128)(2,1)}, f32[1,1024]{1,0:T(1,128)}, f32[6,2048]{1,0:T(8,128)}) custom-call(s32[1,512]{1,0:T(1,128)} %ids_ref.1, f32[6,2048]{1,0:T(8,128)} %proj_ref.1, f32[1,1024]{1,0:T(1,128)} %bitcast.8, bf16[512,2048]{1,0:T(8,128)(2,1)} %bitcast.6, bf16[512,1024]{1,0:T(8,128)(2,1)} %bitcast.7, ...), custom_call_target="tpu_custom_call" | custom-call | tf_op jit(solution)/shard_map/layer/pallas_call | solution.py:537
  105.1 3.9 %hand_over.1 = (bf16[512,2048]{1,0:T(8,128)(2,1)}, f32[3,16,1024]{2,1,0:T(8,128)}, f32[1,1024]{1,0:T(1,128)}, f32[6,2048]{1,0:T(8,128)}) custom-call(bf16[512,2048]{1,0:T(8,128)(2,1)} %get-tuple-element.12.refs_0_, f32[3,16,1024]{2,1,0:T(8,128)} %get-tuple-element.13.refs_1_, f32[1,1024]{1,0:T(1,128)} %get-tuple-element.14.refs_2_, ...), custom_call_target="tpu_custom_call" | custom-call | tf_op jit(solution)/shard_map/hand_over/pallas_call | solution.py:567

commit v4 on v3

--- a/solution.py
+++ b/solution.py
@@ -32,11 +32,11 @@
     return lax.dot_general(a, b, dims, preferred_element_type=F32)
 
 
-def entry_barrier(devices):
+def entry_signal(devices):
     barrier = pltpu.get_barrier_semaphore()
     for device in devices:
         pl.semaphore_signal(barrier, inc=1, device_id=device, device_id_type=MESH)
-    pl.semaphore_wait(barrier, len(devices))
+    return lambda: pl.semaphore_wait(barrier, len(devices))
 
 
 def send(src, dst, ssem, rsem, device):
@@ -77,7 +77,7 @@
     wbuf, wsem, xb, q, k, v, sqk, dkv, og, ogsem, sc, datt, nf, ns, nall, proj3, gain_row,
     xssem, xrsem, gsem, nsem, free_sem,
     blk, pre, sbuf, rbuf, obuf, sssem, srsem,
-    xt_ref, g_ref, igsem, ar, arr, arsem, fs, fr, fsem, rgsem, sems, *scr,
+    xt_ref, g_ref, igsem, ar, arr, arsem, asend, agot, asum, aall, got, gotsem, rgsem, sems, *scr,
 ):
     tr = Trace()
 
@@ -90,7 +90,7 @@
         lax.fori_loop(first // 2, last // 2, two, 0)
 
     tx, t2 = scr[0:6], scr[6:12]
-    recv = [[scr[12 + 18 * phase + 6 * m : 18 + 18 * phase + 6 * m] for m in range(3)] for phase in range(3)]
+    recv = [[scr[12 + 18 * phase + 6 * m : 18 + 18 * phase + 6 * m] for m in range(3)] for phase in range(2)]
     c = lax.axis_index("c")
     peer = {"c": 1 - c}
     y = lax.axis_index("y")
@@ -115,6 +115,11 @@
                 og_hbm.at[:, pl.ds(pl.multiple_of(col + h * DH, DH), DH)], og.at[first + h], ogsem.at[m * 4 + h])
             cp.start()
             ogloads.append(cp)
+
+    plane = [{"z": ring("z", dz), "y": ring("y", dy)} for dz in range(4) for dy in range(4) if dz or dy]
+    plane += [{"x": ring("x", n)} for n in (1, 2, 3)] + [peer]
+    plane += [{a: ring(a, n), "c": 1 - c} for a in ("x", "y", "z") for n in (1, 2, 3)]
+    all_entered = entry_signal(plane)
 
     ids = ids_ref[...].astype(F32)
     nf[...] = jnp.zeros_like(nf)
@@ -135,9 +140,6 @@
     nums = nf[...].astype(BF16)
     numt = jnp.concatenate([nums, nums, nums], axis=0)
 
-    plane = [{"z": ring("z", dz), "y": ring("y", dy)} for dz in range(4) for dy in range(4) if dz or dy]
-    entry_barrier([peer] + plane + [{"x": ring("x", n)} for n in (1, 2, 3)])
-
     tr("inputs")
     xload.wait()
     xcopies = []
@@ -148,6 +150,8 @@
         xb[0, :, cols] = x
         src, dst = tx[2 + j % 4].at[j // 4], recv[0][1 + j // 4][2 + j % 4]
         src[...] = x.astype(F32).reshape(4, 2, 4, 16, 256)
+        if j == 0:
+            all_entered()
         xcopies.append(send(src, dst, xssem.at[j], xrsem.at[j], peer))
     for h in range(4):
         ogloads[2 * h].wait()
@@ -155,23 +159,24 @@
     g_copy = send(dkv.at[0:4], dkv.at[4:8], gsem.at[0], gsem.at[1], peer)
     n_copy = send(nf, ns, nsem.at[0], nsem.at[1], peer)
 
+    def place(n, at, a):
+        if n == 1:
+            v[at] = a.astype(BF16)
+        else:
+            s = 1.0 / (1.0 + jnp.exp(-a))
+            slope = s * (1.0 + a * (1.0 - s))
+            if n == 0:
+                k[at] = (a * s).astype(BF16)
+                sqk[8 + at] = slope
+            else:
+                q[at] = (a * s).astype(BF16)
+                sqk[at] = slope
+
     def project(slot, n, base):
         for half in range(2):
             p = dot(xb[slot], wbuf[n, :, half * 256 : half * 256 + 256])
             for hh in range(2):
-                a = p[:, hh * DH : hh * DH + DH]
-                at = base + half * 2 + hh
-                if n == 1:
-                    v[at] = a.astype(BF16)
-                else:
-                    s = 1.0 / (1.0 + jnp.exp(-a))
-                    slope = s * (1.0 + a * (1.0 - s))
-                    if n == 0:
-                        k[at] = (a * s).astype(BF16)
-                        sqk[8 + at] = slope
-                    else:
-                        q[at] = (a * s).astype(BF16)
-                        sqk[at] = slope
+                place(n, base + half * 2 + hh, p[:, hh * DH : hh * DH + DH])
 
     def kv_step(n):
         blk[0, n // 4, lax.rem(n, 4)] = dot(k[n], v[n], TN)
@@ -187,13 +192,22 @@
     kv_steps(mine)
     for h in range(4):
         ogloads[2 * h + 1].wait()
-    tr("peer_wait")
-    for j in range(8):
-        xcopies[j].wait()
-        xb[1, :, j * 256 : j * 256 + 256] = recv[0][1 + j // 4][2 + j % 4][...].reshape(512, 256).astype(BF16)
     tr("peer_kv")
-    project(1, 0, other)
-    project(1, 1, other)
+    for part in range(2):
+        for j in range(4 * part, 4 * part + 4):
+            xcopies[j].wait()
+            xb[1, :, j * 256 : j * 256 + 256] = recv[0][1 + j // 4][2 + j % 4][...].reshape(512, 256).astype(BF16)
+        ks = slice(part * 1024, part * 1024 + 1024)
+        for n in range(2):
+            for half in range(2):
+                p = dot(xb[1, :, ks], wbuf[n, ks, half * 256 : half * 256 + 256])
+                for hh in range(2):
+                    a = p[:, hh * DH : hh * DH + DH]
+                    h = half * 2 + hh
+                    if part == 0:
+                        dkv[8 + 4 * n + h] = a
+                    else:
+                        place(n, other + h, a + dkv[8 + 4 * n + h])
 
     me = z * 4 + y
     spots = sorted(((dz, dy) for dz in range(4) for dy in range(4) if dz or dy),
@@ -278,8 +292,7 @@
         b = n // 4
         h = lax.rem(n, 4)
         a = dkv[8 + n] + dot(q[n], state(0, b, h))
-        root = jnp.sqrt(jnp.mean(a * a, axis=-1, keepdims=True) + 1e-06)
-        inv = 1.0 / root
+        inv = lax.rsqrt(jnp.mean(a * a, axis=-1, keepdims=True) + 1e-06)
         normed = a * inv
         g = og[n].astype(F32)
         dn = g * gain_ref[:, pl.ds(pl.multiple_of(c * HALF + h * DH, DH), DH)]
@@ -409,7 +422,7 @@
     for h in range(4):
         ar[0, 6:7, pl.ds(pl.multiple_of(c * HALF + h * DH, DH), DH)] = gain_row[h] + gain_row[4 + h]
 
-    steps = [("c", 0)] + [(a, m) for a in ("x", "y", "z") for m in (0, 1)]
+    steps = (("c", 0), ("x", 0), ("x", 1))
 
     def small(n):
         axis, m = steps[n]
@@ -420,7 +433,26 @@
     def small_next(n, cp):
         cp.wait()
         ar[n + 1] = ar[n] + arr[n]
-        return small(n + 1) if n + 1 < 7 else None
+        return small(n + 1) if n + 1 < 3 else None
+
+    def plane_gather():
+        for i in range(16):
+            asend[i] = ar[3, :, i * 128 : i * 128 + 128]
+        agot[me] = asend[me]
+        return to_all(asend, agot, 4)
+
+    def plane_return(sent):
+        for cp in sent:
+            cp.wait()
+        total = agot[0]
+        for i in range(1, 16):
+            total = total + agot[i]
+        asum[...] = total
+        aall[me] = total
+        out = []
+        for o, (dz, dy) in enumerate(spots):
+            out.append(send(asum, aall.at[me], sssem.at[5, o], srsem.at[5, o], {"z": ring("z", dz), "y": ring("y", dy)}))
+        return out
 
     small_copy = small(0)
     pl.semaphore_wait(free_sem, 1)
@@ -468,14 +500,24 @@
         sends[hp, phase, 2].wait_recv()
         return recv[phase][1][hp][...] + recv[phase][2][hp][...]
 
+    def first(hp):
+        go(hp, 1, 0, piece(hp, 1, ring(ORDER[PLAN[hp][0]][1], 2)), PLAN[hp][1])
+
+    def second(hp):
+        d = PLAN[hp][1]
+        go(hp, 1, 1, piece(hp, 1, ring(ORDER[PLAN[hp][0]][1], 3 if d == 1 else 1)), -d)
+
     tr("ph1a")
     for hp in range(6):
-        axis, d = ORDER[PLAN[hp][0]][1], PLAN[hp][1]
         tx[hp][0] = tx[hp][0] + ends(hp, 0)
-        go(hp, 1, 0, piece(hp, 1, ring(axis, 2)), d)
-        go(hp, 1, 1, piece(hp, 1, ring(axis, 3 if d == 1 else 1)), -d)
+        first(hp)
         if hp == 1:
-            small_copy = small_next(2, small_copy)
+            second(0)
+            second(1)
+            small_next(2, small_copy)
+            small_sent = plane_gather()
+    for hp in range(2, 6):
+        second(hp)
     tr("ph1b")
     for hp in range(6):
         axis, d = ORDER[PLAN[hp][0]][1], PLAN[hp][1]
@@ -483,34 +525,37 @@
         via = recv[1][0][hp]
         via[...] = via[...] + piece(hp, 1, ring(axis, 1 if d == 1 else 3))[...]
         go(hp, 1, 2, via, d)
-        if hp == 1:
-            small_copy = small_next(3, small_copy)
-    small_copy = small_next(4, small_copy)
+    small_sent = plane_return(small_sent)
     tr("ph2a")
     for hp in range(6):
-        before, axis = ORDER[PLAN[hp][0]][1:]
-        t2[hp][...] = piece(hp, 1, ring(before, 0))[...] + ends(hp, 1)
-        for m in range(3):
-            sends[hp, 2, m] = send(piece(hp, 2, ring(axis, m + 1)), recv[2][m][hp], sems.at[0, hp, 2, m],
-                                   sems.at[1, hp, 2, m], {axis: ring(axis, m + 1)})
-    small_copy = small_next(5, small_copy)
+        prior, axis = ORDER[PLAN[hp][0]][1:]
+        t2[hp][...] = piece(hp, 1, ring(prior, 0))[...] + ends(hp, 1)
+        for m in (2, 1, 3, 0):
+            for rel in (0, 1) if m else (1,):
+                device = {axis: ring(axis, m), "c": c if rel == 0 else 1 - c} if m else peer
+                if m and rel == 0:
+                    device = {axis: ring(axis, m)}
+                sends[hp, 2, (m, rel)] = send(
+                    piece(hp, 2, ring(axis, m)).at[c if rel == 0 else 1 - c], got.at[hp, rel, m],
+                    gotsem.at[0, hp, rel, m], gotsem.at[1, hp, rel, m], device)
 
     tr("final")
     for hp in range(6):
-        sends[hp, 2, 0].wait_recv()
+        for m in range(4):
+            for rel in (0, 1) if m else (1,):
+                sends[hp, 2, (m, rel)].wait_recv()
         last = ORDER[PLAN[hp][0]][2]
-        fs[:, :, hp * 256 : hp * 256 + 256] = (
-            piece(hp, 2, ring(last, 0))[...] + recv[2][0][hp][...] + ends(hp, 2)
-        ) * scale
-    f_copy = send(fs.at[1 - c], fr, fsem.at[0], fsem.at[1], peer)
-    for t in range(3):
-        wout[t, :, pl.ds(own_col, HALF)] = fs[c, :, t * HALF : t * HALF + HALF]
-    small_next(6, small_copy)
-    code_out[...] = ar[7, 0:6, :] * scale
-    gain_out[...] = ar[7, 6:7, 0 : 2 * HALF] * scale
-    f_copy.wait()
-    for t in range(3):
-        wout[t, :, pl.ds(peer_col, HALF)] = fr[:, t * HALF : t * HALF + HALF]
+        own_sum = piece(hp, 2, ring(last, 0)).at[c][...] + got[hp, 0, 1] + got[hp, 0, 2] + got[hp, 0, 3]
+        peer_sum = got[hp, 1, 0] + got[hp, 1, 1] + got[hp, 1, 2] + got[hp, 1, 3]
+        shift = (hp % 2) * 256
+        wout[hp // 2, :, pl.ds(pl.multiple_of(c * HALF + shift, 256), 256)] = own_sum * scale
+        wout[hp // 2, :, pl.ds(pl.multiple_of((1 - c) * HALF + shift, 256), 256)] = peer_sum * scale
+    for cp in small_sent:
+        cp.wait()
+    for i in range(16):
+        code_out[:, i * 128 : i * 128 + 128] = aall[i, 0:6] * scale
+        if i < 8:
+            gain_out[:, i * 128 : i * 128 + 128] = aall[i, 6:7] * scale
     tr("drain")
     for (hp, phase, m), cp in sends.items():
         if (phase, m) != (0, 0):
@@ -520,8 +565,19 @@
 
 
 def hand_over(*refs):
-    for n in range(4):
-        refs[4 + n][...] = refs[n][...]
+    ins, outs, bufs, sem = refs[:4], refs[4:8], refs[8:12], refs[12]
+    parts = [(0, pl.ds(r * 128, 128)) for r in range(4)] + [(n, slice(None)) for n in (1, 2, 3)]
+    loads = []
+    for i, (n, rows) in enumerate(parts):
+        loads.append(pltpu.make_async_copy(ins[n].at[rows], bufs[n].at[rows], sem.at[0, i]))
+        loads[-1].start()
+    stores = []
+    for i, (n, rows) in enumerate(parts):
+        loads[i].wait()
+        stores.append(pltpu.make_async_copy(bufs[n].at[rows], outs[n].at[rows], sem.at[1, i]))
+        stores[-1].start()
+    for cp in stores:
+        cp.wait()
 
 
 def vmem(*shape, dtype=F32):
@@ -548,29 +604,27 @@
             vmem(16, T), vmem(16, T), vmem(2, 16, T, dtype=BF16), vmem(3, 16, D, dtype=BF16), vmem(8, 1, DH),
             dma((8,)), dma((8,)), dma((2,)), dma((2,)), pltpu.SemaphoreType.REGULAR,
             vmem(2, 2, 4, DH, DH), vmem(2, 16, 32, DH), vmem(2, 16, 32, DH), vmem(2, 16, 32, DH), vmem(2, 16, 32, DH),
-            dma((4, 15)), dma((4, 15)),
+            dma((6, 15)), dma((6, 15)),
             vmem(4, 4, 2, 4, 16, 2 * T, dtype=BF16), vmem(6, 2 * T, 256, dtype=BF16), dma((2,)),
-            vmem(8, 8, D), vmem(7, 8, D), dma((2, 7)),
-            vmem(2, 16, 3 * HALF), vmem(16, 3 * HALF), dma((2,)), dma,
-            dma((2, 6, 3, 3)),
+            vmem(4, 8, D), vmem(3, 8, D), dma((2, 3)),
+            vmem(16, 8, DH), vmem(16, 8, DH), vmem(8, DH), vmem(16, 8, DH),
+            vmem(6, 2, 4, 16, 256), dma((2, 6, 2, 4)), dma,
+            dma((2, 6, 2, 3)),
             *[vmem(2, *DIMS[a], 16, 256) for a, _ in PLAN],
             *[vmem(*DIMS2[a], 16, 256) for a, _ in PLAN],
             *[vmem(*DIMS[a], 16, 256) for _ in range(3) for a, _ in PLAN],
             *[vmem(*DIMS2[a], 16, 256) for _ in range(3) for a, _ in PLAN],
-            *[vmem(2, 16, 256) for _ in range(3) for a, _ in PLAN],
         ],
         compiler_params=pltpu.CompilerParams(collective_id=0, has_side_effects=True, vmem_limit_bytes=67_043_328),
     )(token_ids, code_proj, gain[None], resid[0], out_grad[0], w_query, w_key, w_value)
-    rows = T // 4
-    block = pl.BlockSpec((rows, D), lambda i: (i, 0))
-    whole = [pl.BlockSpec(shape, lambda i, n=len(shape): (0,) * n) for shape in ((3, 16, 2 * HALF), (1, 2 * HALF), (6, D))]
+    shapes = (sds((T, D), BF16), sds((3, 16, 2 * HALF), F32), sds((1, 2 * HALF), F32), sds((6, D), F32))
     resid_grad, w_out, gain_out, code_out = pl.pallas_call(
         hand_over,
         name="hand_over",
-        grid=(4,),
-        out_shape=(sds((T, D), BF16), sds((3, 16, 2 * HALF), F32), sds((1, 2 * HALF), F32), sds((6, D), F32)),
-        in_specs=[block] + whole,
-        out_specs=(block, *whole),
+        out_shape=shapes,
+        in_specs=[any_spec] * 4,
+        out_specs=[any_spec] * 4,
+        scratch_shapes=[*[vmem(*n.shape, dtype=n.dtype) for n in shapes], dma((2, 7))],
     )(resid_grad, w_out, gain_out, code_out)
     return resid_grad[None], w_out.transpose(1, 0, 2), gain_out[0], code_out
 

time: 110 us -> 105 us (0.955)
  Pallas kernels: 108 us -> 103 us
    pallas_call x1, Pallas kernels: 104 us -> 101 us  [body(): pl.pallas_call(functools.partial(kernel, scale), name='layer', out_shape=...]
    pallas_call x1, Pallas kernels: 3.92 us -> 2.55 us  [body(): pl.pallas_call(hand_over, name='hand_over', out_shape=shapes, in_specs=[a...]
where the time goes in v4:
time: 105 us; the launch traced here: 104 us
  Pallas kernels  103 us (98%)
    pallas_call x1, Pallas kernels, body(): pl.pallas_call(functools.partial(kernel, scale), name='layer', out_shape=...  101 us
    pallas_call x1, Pallas kernels, body(): pl.pallas_call(hand_over, name='hand_over', out_shape=shapes, in_specs=[a...  2.55 us

profile of v4, /device:TPU:0, one launch (start us, length us, event | category | flops | bytes accessed | tf_op | source)
XLA Modules:
  0.0 104.2 jit_solution(17973915561782482640)
XLA Ops:
  0.6 100.8 %layer.1 = (f32[3,16,1024]{2,1,0:T(8,128)}, bf16[512,2048]{1,0:T(8,128)(2,1)}, f32[1,1024]{1,0:T(1,128)}, f32[6,2048]{1,0:T(8,128)}) custom-call(s32[1,512]{1,0:T(1,128)} %ids_ref.1, f32[6,2048]{1,0:T(8,128)} %proj_ref.1, f32[1,1024]{1,0:T(1,128)} %bitcast.8, bf16[512,2048]{1,0:T(8,128)(2,1)} %bitcast.6, bf16[512,1024]{1,0:T(8,128)(2,1)} %bitcast.7, ...), custom_call_target="tpu_custom_call" | custom-call | tf_op jit(solution)/shard_map/layer/pallas_call | solution.py:593
  101.5 2.6 %hand_over.1 = (bf16[512,2048]{1,0:T(8,128)(2,1)}, f32[3,16,1024]{2,1,0:T(8,128)}, f32[1,1024]{1,0:T(1,128)}, f32[6,2048]{1,0:T(8,128)}) custom-call(bf16[512,2048]{1,0:T(8,128)(2,1)} %get-tuple-element.12.refs_0_, f32[3,16,1024]{2,1,0:T(8,128)} %get-tuple-element.13.refs_1_, f32[1,1024]{1,0:T(1,128)} %get-tuple-element.14.refs_2_, ...), custom_call_target="tpu_custom_call" | custom-call | tf_op jit(solution)/shard_map/hand_over/pallas_call | solution.py:621

commit v5 on v4

--- a/solution.py
+++ b/solution.py
@@ -72,9 +72,9 @@
 
 
 def kernel(
-    scale, ids_ref, proj_ref, gain_ref, resid_hbm, og_hbm, wq_hbm, wk_hbm, wv_hbm,
+    scale, ids_hbm, proj_hbm, gain_hbm, resid_hbm, og_hbm, wq_hbm, wk_hbm, wv_hbm,
     wout, rg_hbm, gain_out, code_out,
-    wbuf, wsem, xb, q, k, v, sqk, dkv, og, ogsem, sc, datt, nf, ns, nall, proj3, gain_row,
+    ids_ref, proj_ref, gain_ref, opsem, wbuf, wsem, xb, q, k, v, sqk, dkv, og, ogsem, sc, datt, nf, ns, nall, proj3, gain_row,
     xssem, xrsem, gsem, nsem, free_sem,
     blk, pre, sbuf, rbuf, obuf, sssem, srsem,
     xt_ref, g_ref, igsem, ar, arr, arsem, asend, agot, asum, aall, got, gotsem, rgsem, sems, *scr,
@@ -101,26 +101,32 @@
     other = (1 - c) * 4
 
     tr("enter")
-    xload = pltpu.make_async_copy(resid_hbm, xb.at[0], ogsem.at[8])
-    xload.start()
-    loads = []
-    for n, w in enumerate((wk_hbm, wv_hbm, wq_hbm)):
-        cp = pltpu.make_async_copy(w.at[:, pl.ds(own_col, HALF)], wbuf.at[n], wsem.at[n])
-        cp.start()
-        loads.append(cp)
+    small_loads = []
+    for n, (src, dst) in enumerate(((ids_hbm, ids_ref), (proj_hbm, proj_ref), (gain_hbm, gain_ref))):
+        small_loads.append(pltpu.make_async_copy(src, dst, opsem.at[n]))
+        small_loads[-1].start()
+    xloads = []
+    for n in range(4):
+        cols = pl.ds(n * 512, 512)
+        xloads.append(pltpu.make_async_copy(resid_hbm.at[:, cols], xb.at[0, :, cols], opsem.at[3 + n]))
+        xloads[-1].start()
+    loads = [
+        pltpu.make_async_copy(w.at[:, pl.ds(own_col, HALF)], wbuf.at[n], wsem.at[n])
+        for n, w in enumerate((wk_hbm, wv_hbm, wq_hbm))
+    ]
     ogloads = []
     for h in range(4):
         for m, (first, col) in enumerate(((other, peer_col), (mine, own_col))):
-            cp = pltpu.make_async_copy(
-                og_hbm.at[:, pl.ds(pl.multiple_of(col + h * DH, DH), DH)], og.at[first + h], ogsem.at[m * 4 + h])
-            cp.start()
-            ogloads.append(cp)
+            ogloads.append(pltpu.make_async_copy(
+                og_hbm.at[:, pl.ds(pl.multiple_of(col + h * DH, DH), DH)], og.at[first + h], ogsem.at[m * 4 + h]))
 
     plane = [{"z": ring("z", dz), "y": ring("y", dy)} for dz in range(4) for dy in range(4) if dz or dy]
     plane += [{"x": ring("x", n)} for n in (1, 2, 3)] + [peer]
     plane += [{a: ring(a, n), "c": 1 - c} for a in ("x", "y", "z") for n in (1, 2, 3)]
     all_entered = entry_signal(plane)
 
+    for cp in small_loads:
+        cp.wait()
     ids = ids_ref[...].astype(F32)
     nf[...] = jnp.zeros_like(nf)
     rest = jnp.zeros((8, D), F32)
@@ -141,9 +147,13 @@
     numt = jnp.concatenate([nums, nums, nums], axis=0)
 
     tr("inputs")
-    xload.wait()
     xcopies = []
     for j in range(8):
+        if j % 2 == 0:
+            xloads[j // 2].wait()
+        if j == 2:
+            for cp in loads + ogloads:
+                cp.start()
         cols = slice(j * 256, j * 256 + 256)
         add = dot(numt, proj3[:, :, cols].reshape(48, 256), TN)
         x = (xb[0, :, cols].astype(F32) + add).astype(BF16)
@@ -292,11 +302,13 @@
         b = n // 4
         h = lax.rem(n, 4)
         a = dkv[8 + n] + dot(q[n], state(0, b, h))
-        inv = lax.rsqrt(jnp.mean(a * a, axis=-1, keepdims=True) + 1e-06)
-        normed = a * inv
         g = og[n].astype(F32)
         dn = g * gain_ref[:, pl.ds(pl.multiple_of(c * HALF + h * DH, DH), DH)]
-        da = ((dn - normed * jnp.mean(dn * normed, axis=-1, keepdims=True)) * inv).astype(BF16)
+        square = jnp.sum(a * a, axis=-1, keepdims=True)
+        cross = jnp.sum(dn * a, axis=-1, keepdims=True)
+        inv = lax.rsqrt(square * (1.0 / DH) + 1e-06)
+        normed = a * inv
+        da = (dn * inv - normed * ((cross * inv) * (inv * (1.0 / DH)))).astype(BF16)
         datt[n] = da
         gain_row[n] = jnp.sum(g * normed, axis=0, keepdims=True)
         blk[1, b, h] = dot(q[n], da, TN)
@@ -594,12 +606,13 @@
         functools.partial(kernel, scale),
         name="layer",
         out_shape=(sds((3, 16, 2 * HALF), F32), sds((T, D), BF16), sds((1, 2 * HALF), F32), sds((6, D), F32)),
-        in_specs=[vm] * 3 + [any_spec] * 5,
+        in_specs=[any_spec] * 8,
         out_specs=(vm, any_spec, vm, vm),
         scratch_shapes=[
+            vmem(1, T, dtype=jnp.int32), vmem(6, D), vmem(1, 2 * HALF), dma((7,)),
             vmem(3, D, HALF, dtype=BF16), dma((3,)), vmem(2, T, D, dtype=BF16),
             vmem(8, T, DH, dtype=BF16), vmem(8, T, DH, dtype=BF16), vmem(8, T, DH, dtype=BF16),
-            vmem(16, T, DH), vmem(16, T, DH), vmem(8, T, DH, dtype=BF16), dma((9,)),
+            vmem(16, T, DH), vmem(16, T, DH), vmem(8, T, DH, dtype=BF16), dma((8,)),
             vmem(8, T, T, dtype=BF16), vmem(8, T, DH, dtype=BF16),
             vmem(16, T), vmem(16, T), vmem(2, 16, T, dtype=BF16), vmem(3, 16, D, dtype=BF16), vmem(8, 1, DH),
             dma((8,)), dma((8,)), dma((2,)), dma((2,)), pltpu.SemaphoreType.REGULAR,

time: 105 us -> 105 us (level)
  no operation moved by 1% of the time
where the time goes in v5:
time: 105 us; the launch traced here: 103 us
  Pallas kernels  103 us (98%)
    pallas_call x1, Pallas kernels, body(): pl.pallas_call(functools.partial(kernel, scale), name='layer', out_shape=...  100 us
    pallas_call x1, Pallas kernels, body(): pl.pallas_call(hand_over, name='hand_over', out_shape=shapes, in_specs=[a...  2.55 us

profile of v5, /device:TPU:0, one launch (start us, length us, event | category | flops | bytes accessed | tf_op | source)
XLA Modules:
  0.0 103.4 jit_solution(14370383144717300683)
XLA Ops:
  0.6 100.1 %layer.1 = (f32[3,16,1024]{2,1,0:T(8,128)}, bf16[512,2048]{1,0:T(8,128)(2,1)}, f32[1,1024]{1,0:T(1,128)}, f32[6,2048]{1,0:T(8,128)}) custom-call(s32[1,512]{1,0:T(1,128)} %ids_hbm.1, f32[6,2048]{1,0:T(8,128)} %proj_hbm.1, f32[1,1024]{1,0:T(1,128)} %bitcast.8, bf16[512,2048]{1,0:T(8,128)(2,1)} %bitcast.6, bf16[512,1024]{1,0:T(8,128)(2,1)} %bitcast.7, ...), custom_call_target="tpu_custom_call" | custom-call | tf_op jit(solution)/shard_map/layer/pallas_call | solution.py:605
  100.7 2.6 %hand_over.1 = (bf16[512,2048]{1,0:T(8,128)(2,1)}, f32[3,16,1024]{2,1,0:T(8,128)}, f32[1,1024]{1,0:T(1,128)}, f32[6,2048]{1,0:T(8,128)}) custom-call(bf16[512,2048]{1,0:T(8,128)(2,1)} %get-tuple-element.12.refs_0_, f32[3,16,1024]{2,1,0:T(8,128)} %get-tuple-element.13.refs_1_, f32[1,1024]{1,0:T(1,128)} %get-tuple-element.14.refs_2_, ...), custom_call_target="tpu_custom_call" | custom-call | tf_op jit(solution)/shard_map/hand_over/pallas_call | solution.py:634

commit v6 on v5

--- a/solution.py
+++ b/solution.py
@@ -81,13 +81,13 @@
 ):
     tr = Trace()
 
-    def pairs(first, last, step):
-        def two(i, _):
-            step(2 * i)
-            step(2 * i + 1)
+    def pairs(first, last, step, width=2):
+        def several(i, _):
+            for n in range(width):
+                step(width * i + n)
             return 0
 
-        lax.fori_loop(first // 2, last // 2, two, 0)
+        lax.fori_loop(first // width, last // width, several, 0)
 
     tx, t2 = scr[0:6], scr[6:12]
     recv = [[scr[12 + 18 * phase + 6 * m : 18 + 18 * phase + 6 * m] for m in range(3)] for phase in range(2)]
@@ -314,7 +314,7 @@
         blk[1, b, h] = dot(q[n], da, TN)
 
     tr("fwd")
-    pairs(0, 8, forward_step)
+    pairs(0, 8, forward_step, 4)
     sent = scan_start(1)
 
     def put(kind, n, value):
@@ -323,7 +323,8 @@
         g_ref[kind * 2 + h // 2, pl.ds(pl.multiple_of(b * T, T), T),
               pl.ds(pl.multiple_of(lax.rem(h, 2) * DH, DH), DH)] = value.astype(BF16)
 
-    def back_step(n):
+    def back_step(i):
+        n = lax.rem(i, 2) + 4 * lax.rem(i // 2, 2) + 2 * (i // 4)
         b = n // 4
         h = lax.rem(n, 4)
         da = datt[n]
@@ -368,13 +369,15 @@
 
     tr("back1")
     pairs(0, 4, back_step)
+    far((0,))
+    straight((0,))
     tr("scanmid1")
     sent = scan_middle(1, sent)
     tr("back2")
     pairs(4, 8, back_step)
     tr("xfirst")
-    far((0, 1))
-    straight((0, 1))
+    far((1,))
+    straight((1,))
     tr("scanend1")
     scan_end(1, sent)
 
@@ -384,7 +387,7 @@
         put(2, n, dkv[8 + n] + dot(k[n], st))
 
     tr("last")
-    pairs(0, 8, last_step)
+    pairs(0, 8, last_step, 4)
     pl.semaphore_signal(free_sem, inc=1, device_id=peer, device_id_type=MESH)
     tr("yzfirst")
     far((2, 3))

time: 105 us -> 105 us (level)
  no operation moved by 1% of the time
where the time goes in v6:
time: 105 us; the launch traced here: 103 us
  Pallas kernels  103 us (98%)
    pallas_call x1, Pallas kernels, body(): pl.pallas_call(functools.partial(kernel, scale), name='layer', out_shape=...  100 us
    pallas_call x1, Pallas kernels, body(): pl.pallas_call(hand_over, name='hand_over', out_shape=shapes, in_specs=[a...  2.55 us

profile of v6, /device:TPU:0, one launch (start us, length us, event | category | flops | bytes accessed | tf_op | source)
XLA Modules:
  0.0 103.5 jit_solution(17564209268464810397)
XLA Ops:
  0.6 100.1 %layer.1 = (f32[3,16,1024]{2,1,0:T(8,128)}, bf16[512,2048]{1,0:T(8,128)(2,1)}, f32[1,1024]{1,0:T(1,128)}, f32[6,2048]{1,0:T(8,128)}) custom-call(s32[1,512]{1,0:T(1,128)} %ids_hbm.1, f32[6,2048]{1,0:T(8,128)} %proj_hbm.1, f32[1,1024]{1,0:T(1,128)} %bitcast.8, bf16[512,2048]{1,0:T(8,128)(2,1)} %bitcast.6, bf16[512,1024]{1,0:T(8,128)(2,1)} %bitcast.7, ...), custom_call_target="tpu_custom_call" | custom-call | tf_op jit(solution)/shard_map/layer/pallas_call | solution.py:608
  100.8 2.6 %hand_over.1 = (bf16[512,2048]{1,0:T(8,128)(2,1)}, f32[3,16,1024]{2,1,0:T(8,128)}, f32[1,1024]{1,0:T(1,128)}, f32[6,2048]{1,0:T(8,128)}) custom-call(bf16[512,2048]{1,0:T(8,128)(2,1)} %get-tuple-element.12.refs_0_, f32[3,16,1024]{2,1,0:T(8,128)} %get-tuple-element.13.refs_1_, f32[1,1024]{1,0:T(1,128)} %get-tuple-element.14.refs_2_, ...), custom_call_target="tpu_custom_call" | custom-call | tf_op jit(solution)/shard_map/hand_over/pallas_call | solution.py:637

commit v7 on v6

--- a/solution.py
+++ b/solution.py
@@ -515,16 +515,24 @@
         sends[hp, phase, 2].wait_recv()
         return recv[phase][1][hp][...] + recv[phase][2][hp][...]
 
+    def gather(hp, i):
+        p = piece(hp, 1, i)
+        two, three = ((r.at[:, :, i] if PLAN[hp][0] == "y" else r.at[i]) for r in (recv[0][1][hp], recv[0][2][hp]))
+        p[...] = p[...] + two[...] + three[...]
+
     def first(hp):
+        sends[hp, 0, 1].wait_recv()
+        sends[hp, 0, 2].wait_recv()
+        gather(hp, ring(ORDER[PLAN[hp][0]][1], 2))
         go(hp, 1, 0, piece(hp, 1, ring(ORDER[PLAN[hp][0]][1], 2)), PLAN[hp][1])
 
     def second(hp):
         d = PLAN[hp][1]
+        gather(hp, ring(ORDER[PLAN[hp][0]][1], 3 if d == 1 else 1))
         go(hp, 1, 1, piece(hp, 1, ring(ORDER[PLAN[hp][0]][1], 3 if d == 1 else 1)), -d)
 
     tr("ph1a")
     for hp in range(6):
-        tx[hp][0] = tx[hp][0] + ends(hp, 0)
         first(hp)
         if hp == 1:
             second(0)
@@ -536,6 +544,8 @@
     tr("ph1b")
     for hp in range(6):
         axis, d = ORDER[PLAN[hp][0]][1], PLAN[hp][1]
+        gather(hp, ring(axis, 1 if d == 1 else 3))
+        gather(hp, ring(axis, 0))
         sends[hp, 1, 0].wait_recv()
         via = recv[1][0][hp]
         via[...] = via[...] + piece(hp, 1, ring(axis, 1 if d == 1 else 3))[...]

time: 105 us -> 104 us (level)
  no operation moved by 1% of the time
where the time goes in v7:
time: 104 us; the launch traced here: 103 us
  Pallas kernels  103 us (99%)
    pallas_call x1, Pallas kernels, body(): pl.pallas_call(functools.partial(kernel, scale), name='layer', out_shape=...  100 us
    pallas_call x1, Pallas kernels, body(): pl.pallas_call(hand_over, name='hand_over', out_shape=shapes, in_specs=[a...  2.55 us

profile of v7, /device:TPU:0, one launch (start us, length us, event | category | flops | bytes accessed | tf_op | source)
XLA Modules:
  0.0 103.4 jit_solution(16644134827018792955)
XLA Ops:
  0.6 100.0 %layer.1 = (f32[3,16,1024]{2,1,0:T(8,128)}, bf16[512,2048]{1,0:T(8,128)(2,1)}, f32[1,1024]{1,0:T(1,128)}, f32[6,2048]{1,0:T(8,128)}) custom-call(s32[1,512]{1,0:T(1,128)} %ids_hbm.1, f32[6,2048]{1,0:T(8,128)} %proj_hbm.1, f32[1,1024]{1,0:T(1,128)} %bitcast.8, bf16[512,2048]{1,0:T(8,128)(2,1)} %bitcast.6, bf16[512,1024]{1,0:T(8,128)(2,1)} %bitcast.7, ...), custom_call_target="tpu_custom_call" | custom-call | tf_op jit(solution)/shard_map/layer/pallas_call | solution.py:618
  100.6 2.6 %hand_over.1 = (bf16[512,2048]{1,0:T(8,128)(2,1)}, f32[3,16,1024]{2,1,0:T(8,128)}, f32[1,1024]{1,0:T(1,128)}, f32[6,2048]{1,0:T(8,128)}) custom-call(bf16[512,2048]{1,0:T(8,128)(2,1)} %get-tuple-element.12.refs_0_, f32[3,16,1024]{2,1,0:T(8,128)} %get-tuple-element.13.refs_1_, f32[1,1024]{1,0:T(1,128)} %get-tuple-element.14.refs_2_, ...), custom_call_target="tpu_custom_call" | custom-call | tf_op jit(solution)/shard_map/hand_over/pallas_call | solution.py:647
